TPU v7x, 512 devices: a whole 4x8x8 slice. The times are simulated.
512 devices in a mesh: orb: 32 (over z, x_lo, core), spx: 16 (over x_hi, y).
Axes of the slice: x: 4 (x_hi: 2, x_lo: 2; x = x_hi * 2 + x_lo), y: 8, z: 8, core: 2. Of those that a mesh axis runs over, the one named last changes fastest.
Arguments:
- weights: float32 [131072], P('orb'), may hold values from 0.25 to 2
- losvd: bfloat16 [131072, 128, 64], P('orb', 'spx'), may hold values from 0 to 0.00390625
- occupancy: int32 [1024, 128], P('orb', 'spx'), may hold values 0 or 1
- template_of: int32 [131072], P('orb'), may hold values from 0 to 255
- templates: bfloat16 [256, 4160], P('orb'), may hold values from -0.046875 to 0.046875
- observed: float32 [128, 4096], P('spx'), may hold values from -6 to 6
- inv_sigma: float32 [128, 4096], P('spx'), may hold values from 0.5 to 2
Outputs:
- weights_next: float32 [131072], P('orb')
- residual: float32 [128, 4096], P('spx')
All inputs are finite; a program needn't handle non-finite values. No bound on the sum of `occupancy` on one device may be relied on, other than what follows from the above.
Results may differ from a plain program's by a relative error of at most 0.0005.
Values may be sent and summed in bfloat16 or wider, within the bound.
No kernel may reach another device: no remote copies, remote signals or barrier semaphores. Data moves between devices by JAX's collectives and lax.ppermute only.
A program may use at most 64 MiB of HBM per device.

v0:
```python
import jax
import jax.numpy as jnp
from jax import lax
from jax.sharding import PartitionSpec as P

step_size = 0.5


def cut_along(array, dim, size):
    shape = array.shape
    tiles = array.reshape(*shape[:dim], size, shape[dim] // size, *shape[dim + 1 :])
    return jnp.moveaxis(tiles, dim, 0)


def sum_at_owner(array, axis, dim):
    size = lax.axis_size(axis)
    tiles = lax.all_to_all(cut_along(array, dim, size), axis, 0, 0, tiled=True)
    return jnp.sum(tiles, axis=0)


def copy_for_each(array, axis):
    copies = jnp.broadcast_to(array, (lax.axis_size(axis), *array.shape))
    return lax.all_to_all(copies, axis, split_axis=0, concat_axis=0, tiled=True)


def in_order(tiles, dim):
    tiles = jnp.moveaxis(tiles, 0, dim)
    shape = tiles.shape
    return tiles.reshape(*shape[:dim], shape[dim] * shape[dim + 1], *shape[dim + 2 :])


def gathered_copies(array, axis, dim):
    tiles = copy_for_each(array, axis)
    return in_order(tiles, dim)


def of_everyone(array, axis):
    return copy_for_each(array, axis).sum(axis=0)


def local(weights, losvd, occupancy, template_of, templates, observed, inv_sigma):
    orbit_count, spaxel_count, velocity_bins = losvd.shape
    block_count = occupancy.shape[0]
    block_size = orbit_count // block_count
    local_templates = templates.shape[0]
    wavelengths = observed.shape[1]
    template_total = local_templates * lax.axis_size("orb")
    occupied = occupancy.astype(jnp.bfloat16)
    masked = (
        losvd.reshape(block_count, block_size, spaxel_count, velocity_bins)
        * occupied[:, None, :, None]
    ).reshape(orbit_count, spaxel_count * velocity_bins)
    template_range = jnp.arange(template_total, dtype=jnp.int32)
    onehot = (template_of[:, None] == template_range[None, :]).astype(jnp.bfloat16)
    shifted = jnp.stack(
        [templates[:, offset : offset + wavelengths] for offset in range(velocity_bins)], axis=1
    )
    shifted_wide = shifted.astype(jnp.float32)
    current = weights
    residual = None
    assign = onehot * current.astype(jnp.bfloat16)[:, None]

    def partial_mix(first_row, row_count, assign=assign):
        return lax.dot_general(
            assign, masked, (((0,), (0,)), ((), ())), preferred_element_type=jnp.float32
        )

    mixed = sum_at_owner(
        partial_mix(jnp.int32(0), local_templates * lax.axis_size("orb")), "orb", 0
    )
    mixture = mixed.reshape(local_templates, spaxel_count, velocity_bins)
    model_part = jnp.einsum(
        "tsv,tvw->sw",
        mixture,
        shifted_wide,
        preferred_element_type=jnp.float32,
        precision=lax.Precision.HIGHEST,
    )
    share = wavelengths // lax.axis_size("orb")
    model_share = sum_at_owner(model_part, "orb", 1)
    first_bin = lax.axis_index("orb") * share
    observed_share = lax.dynamic_slice_in_dim(observed, first_bin, share, 1)
    sigma_share = lax.dynamic_slice_in_dim(inv_sigma, first_bin, share, 1)
    residual_share = (model_share - observed_share) * sigma_share
    scaled = gathered_copies((residual_share * sigma_share).astype(jnp.bfloat16), "orb", 1)
    residual = gathered_copies(residual_share, "orb", 1)
    response = jnp.einsum("tvw,sw->tsv", shifted, scaled, preferred_element_type=jnp.float32)
    response = response.astype(jnp.bfloat16).reshape(local_templates, spaxel_count * velocity_bins)
    table = gathered_copies(response, "orb", 0)
    scores = lax.dot_general(
        masked, table, (((1,), (1,)), ((), ())), preferred_element_type=jnp.float32
    )
    gradient_part = jnp.sum(scores * onehot.astype(jnp.float32), axis=1)
    gradient = of_everyone(gradient_part, "spx")
    current = jnp.maximum(current - step_size * gradient, 0.0)
    return (current, residual)


def solution(mesh):
    placed = (
        P("orb"),
        P("orb", "spx", None),
        P("orb", "spx"),
        P("orb"),
        P("orb", None),
        P("spx", None),
        P("spx", None),
    )
    return jax.shard_map(
        local, mesh=mesh, in_specs=placed, out_specs=(P("orb"), P("spx", None)), check_vma=False
    )
```

profile of v0, /device:TPU:8, one launch (start us, length us, event | category | flops | bytes accessed | tf_op | source)
XLA Modules:
  0.0 175.1 jit_solution(6576473276913954668)
XLA Ops:
  2.3 2.5 %broadcast_multiply_fusion = bf16[4096,8,64]{0,2,1:T(8,128)(2,1)S(1)} fusion(bf16[4096,8,64]{0,2,1:T(8,128)(2,1)} %param.8, bf16[4096,8]{0,1:T(8,128)(2,1)S(1)} %broadcast_bitcast_fusion), kind=kLoop, calls=%fused_computation.10 | loop fusion | flops 2097152 | bytes 8454144 | tf_op jit(solution)/shard_map/mul | solution.py:50
  4.8 1.9 %copy-done.1 = bf16[4096,8,64]{0,2,1:T(8,128)(2,1)} copy-done((bf16[4096,8,64]{0,2,1:T(8,128)(2,1)}, bf16[4096,8,64]{0,2,1:T(8,128)(2,1)S(1)}, u32[]{:S(2)}) %copy-start.1) | copy-done | bytes 4194328
  6.7 2.1 %fusion.4 = f32[32,8,512]{2,1,0:T(8,128)} fusion(bf16[4096,512,1]{0,1,2:T(8,128)(2,1)S(1)} %bitcast.167, s32[32,8]{1,0:T(8,128)S(1)} %multiply_add_fusion, s32[4096]{0:T(1024)S(1)} %copy-done.3, bf16[4096]{0:T(1024)(128)(2,1)S(1)} %convert_element_type.23), kind=kOutput, calls=%fused_computation.7 | convolution fusion | flops 1075838976 | bytes 4744192 | tf_op jit(solution)/shard_map/dot_general | solution.py:64
  8.8 11.6 %all-to-all-start = ((f32[32,8,512]{2,1,0:T(8,128)}), f32[32,8,512]{2,1,0:T(8,128)S(1)}, u32[]{:S(2)}, u32[]{:S(2)}) async-start(f32[32,8,512]{2,1,0:T(8,128)} %fusion.4), calls=%async_computation | async-start | bytes 1048576 | tf_op jit(solution)/shard_map/all_to_all | solution.py:17
  28.6 0.8 copy.182
  38.3 0.8 copy.195
  39.1 0.8 copy.196
  42.1 0.8 copy.200
  50.5 0.8 copy.147
  52.0 0.8 copy.149
  52.8 0.8 copy.150
  55.8 27.7 %stack.259 = bf16[8,64,4096]{2,1,0:T(8,128)(2,1)} concatenate(bf16[8,1,4096]{2,1,0:T(2,128)(2,1)} %copy.147, bf16[8,1,4096]{2,1,0:T(2,128)(2,1)} %copy.148, bf16[8,1,4096]{2,1,0:T(2,128)(2,1)} %copy.149, bf16[8,1,4096]{2,1,0:T(2,128)(2,1)} %copy.150, bf16[8,1,4096]{2,1,0:T(2,128)(2,1)} %copy.151, bf16[8,1,4096]{2,1,0:T(2,128)(2,1)} %copy.152, bf16[8,1,4096]{2,1,0:T(2,128)(2,1)} %copy.153, ...), dimensions={1} | concatenate | bytes 8388608 | tf_op jit(solution)/shard_map/stack | solution.py:55
  83.6 4.2 %fusion.8 = f32[32,8,128]{2,1,0:T(8,128)} fusion(f32[8,8,64,1]{2,1,0,3:T(8,128)S(1)} %reshape.67, bf16[8,64,4096]{2,1,0:T(8,128)(2,1)} %stack.259), kind=kOutput, calls=%fused_computation.12 | convolution fusion | flops 201326592 | bytes 4341760 | tf_op jit(solution)/shard_map/tsv,tvw->sw/dot_general | solution.py:72
  87.8 8.3 %all-to-all-start.1 = ((f32[32,8,128]{2,1,0:T(8,128)}), f32[32,8,128]{2,1,0:T(8,128)S(1)}, u32[]{:S(2)}, u32[]{:S(2)}) async-start(f32[32,8,128]{2,1,0:T(8,128)} %fusion.8), calls=%async_computation.1 | async-start | bytes 262144 | tf_op jit(solution)/shard_map/all_to_all | solution.py:17
  96.1 9.4 %all-to-all-done.1 = f32[32,8,128]{2,1,0:T(8,128)S(1)} async-done(((f32[32,8,128]{2,1,0:T(8,128)}), f32[32,8,128]{2,1,0:T(8,128)S(1)}, u32[]{:S(2)}, u32[]{:S(2)}) %all-to-all-start.1) | async-done | bytes 131104 | tf_op jit(solution)/shard_map/all_to_all | solution.py:17
  106.3 11.5 %all_to_all.31 = bf16[32,8,128]{2,1,0:T(8,128)(2,1)S(1)} all-to-all(bf16[32,8,128]{2,1,0:T(8,128)(2,1)S(1)} %broadcast_in_dim.16), channel_id=1, replica_groups=mesh['orb'=32,'spx'=16] {'orb'}, dimensions={0} | all-to-all | bytes 131072 | tf_op jit(solution)/shard_map/all_to_all | solution.py:23
  117.8 3.9 %fusion.11 = bf16[8,8,64]{2,1,0:T(8,128)(2,1)S(1)} fusion(bf16[8,64,4096]{2,1,0:T(8,128)(2,1)} %stack.259, bf16[32,8,128]{2,1,0:T(8,128)(2,1)S(1)} %all_to_all.31), kind=kOutput, calls=%fused_computation.14 | convolution fusion | flops 33558528 | bytes 4268032 | tf_op jit(solution)/shard_map/tvw,sw->tsv/dot_general | solution.py:87
  121.9 15.3 %all_to_all.32 = bf16[32,8,512]{2,1,0:T(8,128)(2,1)S(1)} all-to-all(bf16[32,8,512]{2,1,0:T(8,128)(2,1)S(1)} %broadcast_in_dim.17), channel_id=1, replica_groups=mesh['orb'=32,'spx'=16] {'orb'}, dimensions={0} | all-to-all | bytes 524288 | tf_op jit(solution)/shard_map/all_to_all | solution.py:23
  137.9 3.9 %all-to-all-start.5 = ((f32[32,8,128]{2,1,0:T(8,128)}), f32[32,8,128]{2,1,0:T(8,128)S(1)}, u32[]{:S(2)}, u32[]{:S(2)}) async-start(f32[32,8,128]{2,1,0:T(8,128)} %broadcast_in_dim.19), calls=%async_computation.5 | async-start | bytes 262144 | tf_op jit(solution)/shard_map/all_to_all | solution.py:23
  141.7 3.5 %fusion.7 = f32[4096]{0:T(1024)S(1)} fusion(s32[4096]{0:T(1024)S(1)} %copy-done.3, bf16[4096,512]{0,1:T(8,128)(2,1)} %bitcast.168, bf16[32,8,512]{2,1,0:T(8,128)(2,1)S(1)} %all_to_all.32), kind=kOutput, calls=%fused_computation.11 | convolution fusion | flops 1078980608 | bytes 4489216 | tf_op jit(solution)/shard_map/dot_general | solution.py:90
  145.2 6.0 %all-to-all-done.5 = f32[32,8,128]{2,1,0:T(8,128)S(1)} async-done(((f32[32,8,128]{2,1,0:T(8,128)}), f32[32,8,128]{2,1,0:T(8,128)S(1)}, u32[]{:S(2)}, u32[]{:S(2)}) %all-to-all-start.5) | async-done | bytes 131104 | tf_op jit(solution)/shard_map/all_to_all | solution.py:23
  151.3 0.9 broadcast_in_dim.18
  152.2 9.7 %all-to-all-start.4 = ((f32[16,1,4096]{2,1,0:T(1,128)}), f32[16,1,4096]{2,1,0:T(1,128)S(1)}, u32[]{:S(2)}, u32[]{:S(2)}) async-start(f32[16,1,4096]{2,1,0:T(1,128)} %broadcast_in_dim.18), calls=%async_computation.4 | async-start | bytes 524288 | tf_op jit(solution)/shard_map/all_to_all | solution.py:23
  161.9 11.8 %all-to-all-done.4 = f32[16,1,4096]{2,1,0:T(1,128)S(1)} async-done(((f32[16,1,4096]{2,1,0:T(1,128)}), f32[16,1,4096]{2,1,0:T(1,128)S(1)}, u32[]{:S(2)}, u32[]{:S(2)}) %all-to-all-start.4) | async-done | bytes 262176 | tf_op jit(solution)/shard_map/all_to_all | solution.py:23
  (85 shorter events, 34.5 us)
Async XLA Ops:
  2.3 4.5 %copy-start.3 = (s32[4096]{0:T(1024)S(1)}, s32[4096]{0:T(1024)}, u32[]{:S(2)}) copy-start(s32[4096]{0:T(1024)} %param.10) | copy-start | bytes 49156
  4.8 1.9 %copy-start.1 = (bf16[4096,8,64]{0,2,1:T(8,128)(2,1)}, bf16[4096,8,64]{0,2,1:T(8,128)(2,1)S(1)}, u32[]{:S(2)}) copy-start(bf16[4096,8,64]{0,2,1:T(8,128)(2,1)S(1)} %broadcast_multiply_fusion) | copy-start | bytes 12582916
  6.7 13.8 %copy-start = (bf16[8,4160]{1,0:T(8,128)(2,1)S(1)}, bf16[8,4160]{1,0:T(8,128)(2,1)}, u32[]{:S(2)}) copy-start(bf16[8,4160]{1,0:T(8,128)(2,1)} %param.11) | copy-start | bytes 199684
  8.8 74.6 %all-to-all-start = ((f32[32,8,512]{2,1,0:T(8,128)}), f32[32,8,512]{2,1,0:T(8,128)S(1)}, u32[]{:S(2)}, u32[]{:S(2)}) async-start(f32[32,8,512]{2,1,0:T(8,128)} %fusion.4), calls=%async_computation | async-start | bytes 1048576 | tf_op jit(solution)/shard_map/all_to_all | solution.py:17
  87.8 17.7 %all-to-all-start.1 = ((f32[32,8,128]{2,1,0:T(8,128)}), f32[32,8,128]{2,1,0:T(8,128)S(1)}, u32[]{:S(2)}, u32[]{:S(2)}) async-start(f32[32,8,128]{2,1,0:T(8,128)} %fusion.8), calls=%async_computation.1 | async-start | bytes 262144 | tf_op jit(solution)/shard_map/all_to_all | solution.py:17
  137.9 13.4 %all-to-all-start.5 = ((f32[32,8,128]{2,1,0:T(8,128)}), f32[32,8,128]{2,1,0:T(8,128)S(1)}, u32[]{:S(2)}, u32[]{:S(2)}) async-start(f32[32,8,128]{2,1,0:T(8,128)} %broadcast_in_dim.19), calls=%async_computation.5 | async-start | bytes 262144 | tf_op jit(solution)/shard_map/all_to_all | solution.py:23
  141.7 32.1 %copy-start.2 = (f32[4096]{0:T(1024)S(1)}, f32[4096]{0:T(1024)}, u32[]{:S(2)}) copy-start(f32[4096]{0:T(1024)} %param.7) | copy-start | bytes 49156
  152.2 21.5 %all-to-all-start.4 = ((f32[16,1,4096]{2,1,0:T(1,128)}), f32[16,1,4096]{2,1,0:T(1,128)S(1)}, u32[]{:S(2)}, u32[]{:S(2)}) async-start(f32[16,1,4096]{2,1,0:T(1,128)} %broadcast_in_dim.18), calls=%async_computation.4 | async-start | bytes 524288 | tf_op jit(solution)/shard_map/all_to_all | solution.py:23
where the time goes:
time: 177 us; the launch traced here: 175 us
  local copies, waits for them, and re-layouts  67.3 us (38%)
  starting transfers between devices  33.5 us (19%)
  waiting for transfers between devices  27.2 us (15%)
  blocking collectives  26.9 us (15%)
  matrix products  13.7 us (8%)
  other arithmetic  5.51 us (3%)
    another operation x69, local copies, waits for them, and re-layouts, local(): jnp.stack([templates[:, offset:offset + wavelengths] for offset in range(...  62.8 us
    all_to_all x2, blocking collectives, copy_for_each(): return lax.all_to_all(copies, axis, split_axis=0, concat_axis=0, tiled=True)  26.9 us
    all_to_all x2, starting transfers between devices, sum_at_owner(): tiles = lax.all_to_all(cut_along(array, dim, size), axis, 0, 0, tiled=True)  19.9 us
    all_to_all x2, waiting for transfers between devices, copy_for_each(): return lax.all_to_all(copies, axis, split_axis=0, concat_axis=0, tiled=True)  17.8 us
    all_to_all x2, starting transfers between devices, copy_for_each(): return lax.all_to_all(copies, axis, split_axis=0, concat_axis=0, tiled=True)  13.6 us
    all_to_all x2, waiting for transfers between devices, sum_at_owner(): tiles = lax.all_to_all(cut_along(array, dim, size), axis, 0, 0, tiled=True)  9.43 us
    dot_general x1, matrix products, local(): jnp.einsum('tsv,tvw->sw', mixture, shifted_wide, preferred_element_type=j...  4.19 us
    dot_general x1, matrix products, local(): jnp.einsum('tvw,sw->tsv', shifted, scaled, preferred_element_type=jnp.flo...  3.91 us
  transfers between devices with their start and end apart: 4, of which 3 were waited for; matrix products, arithmetic and copies ran while one was open for 38% of the time, Pallas kernels for 0%

commit v1 on v0

v1 whole, which is shorter than its diff:
```python
import functools

import jax
import jax.numpy as jnp
from jax import lax
from jax.experimental import pallas as pl
from jax.experimental.pallas import tpu as pltpu
from jax.sharding import PartitionSpec as P

step_size = 0.5

GROUPS = 4
MEMBERS = 8
LANES = 128
VBINS = 64
WAVE = 4096
TWAVE = 4160
WIDE = 4224
TEMPL = 256
PAIR = 128
MIX_CHUNK = 1024
GRAD_CHUNK = 1024


def permuted(ids):
    return ((ids >> 3) & 7) * 32 + (ids >> 6) * 8 + (ids & 7)


def masked_rows(losvd_ref, occ_ref, chunk, step):
    blocks = chunk // LANES
    first = step * blocks
    block = lax.broadcasted_iota(jnp.int32, (occ_ref.shape[1], chunk), 0)
    orbit = lax.broadcasted_iota(jnp.int32, (occ_ref.shape[1], chunk), 1)
    spread = (block == first + orbit // LANES).astype(jnp.bfloat16)
    mask = jnp.dot(
        occ_ref[...].astype(jnp.bfloat16), spread, preferred_element_type=jnp.float32
    ).astype(jnp.bfloat16)
    rows = []
    for s in range(8):
        rows.append(losvd_ref[s] * jnp.broadcast_to(mask[s : s + 1, :], (VBINS, chunk)))
    return rows


def mix_kernel(losvd_ref, occ_ref, ids_ref, weights_ref, out_ref, acc_ref):
    step = pl.program_id(0)
    masked = jnp.concatenate(masked_rows(losvd_ref, occ_ref, MIX_CHUNK, step), axis=0)
    parts = []
    row = lax.broadcasted_iota(jnp.int32, (TEMPL, LANES), 0)
    for b in range(MIX_CHUNK // LANES):
        ids = permuted(ids_ref[b : b + 1, :])
        wide = weights_ref[b : b + 1, :].astype(jnp.bfloat16).astype(jnp.float32)
        parts.append(jnp.where(row == ids, wide, 0.0).astype(jnp.bfloat16))
    assign = jnp.concatenate(parts, axis=1)
    part = lax.dot_general(
        assign, masked, (((1,), (1,)), ((), ())), preferred_element_type=jnp.float32
    )

    @pl.when(step == 0)
    def _():
        acc_ref[...] = part

    @pl.when(step > 0)
    def _():
        acc_ref[...] += part

    @pl.when(step == pl.num_programs(0) - 1)
    def _():
        for k in range(GROUPS):
            for p in range(MEMBERS):
                out_ref[8 * k + p] = acc_ref[32 * p : 32 * p + 32, PAIR * k : PAIR * k + PAIR]


def mix(losvd, occ, ids, weights):
    steps = 4096 // MIX_CHUNK
    rows = MIX_CHUNK // LANES
    return pl.pallas_call(
        mix_kernel,
        name="mix",
        grid=(steps,),
        in_specs=[
            pl.BlockSpec((8, VBINS, MIX_CHUNK), lambda i: (0, 0, i)),
            pl.BlockSpec((8, 32), lambda i: (0, 0)),
            pl.BlockSpec((rows, LANES), lambda i: (i, 0)),
            pl.BlockSpec((rows, LANES), lambda i: (i, 0)),
        ],
        out_specs=pl.BlockSpec((32, 32, PAIR), lambda i: (0, 0, 0)),
        out_shape=jax.ShapeDtypeStruct((32, 32, PAIR), jnp.float32),
        scratch_shapes=[pltpu.VMEM((TEMPL, 8 * VBINS), jnp.float32)],
        compiler_params=pltpu.CompilerParams(vmem_limit_bytes=24 << 20),
        cost_estimate=pl.CostEstimate(flops=1 << 30, bytes_accessed=5 << 20, transcendentals=0),
    )(losvd, occ, ids, weights)


def three_terms(x):
    high = x.astype(jnp.bfloat16)
    rest = x - high.astype(jnp.float32)
    middle = rest.astype(jnp.bfloat16)
    low = (rest - middle.astype(jnp.float32)).astype(jnp.bfloat16)
    return jnp.concatenate([high, middle, low], axis=0)


def model_kernel(shares_ref, templates_ref, out_ref, wide_ref):
    mixture = shares_ref[0]
    for source in range(1, 32):
        mixture = mixture + shares_ref[source]
    terms = three_terms(mixture)
    templates = templates_ref[...].reshape(32, TWAVE)
    tripled = jnp.concatenate([templates, templates, templates], axis=0)
    over_templates = (((0,), (0,)), ((), ()))
    wide_ref[:, :WAVE] = lax.dot_general(
        terms, tripled[:, :WAVE], over_templates, preferred_element_type=jnp.float32
    )
    wide_ref[:, WAVE:TWAVE] = lax.dot_general(
        terms, tripled[:, WAVE:], over_templates, preferred_element_type=jnp.float32
    )
    for s in range(2):
        rows = wide_ref[VBINS * s : VBINS * s + VBINS, :]
        for half in (32, 16, 8):
            rows = rows[:half] + pltpu.roll(rows[half : 2 * half], WIDE - half, 1)
        for half in (4, 2, 1):
            rows = rows + pltpu.roll(pltpu.roll(rows, 8 - half, 0), WIDE - half, 1)
        for q in range(4):
            piece = rows[0:1, 1024 * q : 1024 * q + 1024]
            for member in range(MEMBERS):
                out_ref[member, 4 * s + q : 4 * s + q + 1, :] = piece


def model(shares, templates):
    return pl.pallas_call(
        model_kernel,
        name="model",
        out_shape=jax.ShapeDtypeStruct((MEMBERS, 8, 1024), jnp.float32),
        scratch_shapes=[pltpu.VMEM((PAIR, WIDE), jnp.float32)],
        compiler_params=pltpu.CompilerParams(vmem_limit_bytes=24 << 20),
        cost_estimate=pl.CostEstimate(flops=1 << 27, bytes_accessed=1 << 20, transcendentals=0),
    )(shares, templates)


def respond_kernel(place_ref, parts_ref, observed_ref, sigma_ref, templates_ref, out_ref, res_ref, shift_ref):
    k = place_ref[0]
    p = place_ref[1]
    total = parts_ref[0]
    for member in range(1, MEMBERS):
        total = total + parts_ref[member]
    templates = templates_ref[...].reshape(32, TWAVE)
    for s in range(2):
        spectrum = jnp.concatenate([total[4 * s + q : 4 * s + q + 1, :] for q in range(4)], axis=1)
        inverse = sigma_ref[pl.ds(2 * k + s, 1), :]
        residual = (spectrum - observed_ref[pl.ds(2 * k + s, 1), :]) * inverse
        res_ref[s : s + 1, :] = residual
        scaled = (residual * inverse).astype(jnp.bfloat16).astype(jnp.float32)
        padded = jnp.concatenate([scaled, jnp.zeros((1, WIDE - WAVE), jnp.float32)], axis=1)
        spread = jnp.broadcast_to(padded, (VBINS, WIDE))
        shift_ref[VBINS * s : VBINS * s + VBINS, :] = pltpu.roll(
            spread, 0, 1, stride=1, stride_axis=0
        ).astype(jnp.bfloat16)
    over_waves = (((1,), (1,)), ((), ()))
    response = lax.dot_general(
        templates[:, :WAVE], shift_ref[:, :WAVE], over_waves, preferred_element_type=jnp.float32
    )
    response = response + lax.dot_general(
        templates[:, WAVE:], shift_ref[:, WAVE:TWAVE], over_waves, preferred_element_type=jnp.float32
    )
    share = res_ref[:, pl.ds(pl.multiple_of(p * 512, 512), 512)]
    share = jnp.concatenate([share[:, LANES * j : LANES * j + LANES] for j in range(4)], axis=0)
    high = share.astype(jnp.bfloat16)
    low = (share - high.astype(jnp.float32)).astype(jnp.bfloat16)
    message = jnp.concatenate([response.astype(jnp.bfloat16), high, low], axis=0)
    for target in range(32):
        out_ref[target] = message


def respond(place, parts, observed, sigma, templates):
    vmem = pl.BlockSpec(memory_space=pltpu.VMEM)
    return pl.pallas_call(
        respond_kernel,
        name="respond",
        in_specs=[pl.BlockSpec(memory_space=pltpu.SMEM), vmem, vmem, vmem, vmem],
        out_shape=jax.ShapeDtypeStruct((32, 48, PAIR), jnp.bfloat16),
        scratch_shapes=[
            pltpu.VMEM((2, WAVE), jnp.float32),
            pltpu.VMEM((PAIR, WIDE), jnp.bfloat16),
        ],
        compiler_params=pltpu.CompilerParams(vmem_limit_bytes=24 << 20),
        cost_estimate=pl.CostEstimate(flops=1 << 27, bytes_accessed=1 << 20, transcendentals=0),
    )(place, parts, observed, sigma, templates)


def grad_kernel(losvd_ref, occ_ref, ids_ref, message_ref, out_ref, res_ref, table_ref):
    step = pl.program_id(0)

    @pl.when(step == 0)
    def _():
        for k in range(GROUPS):
            table_ref[:, PAIR * k : PAIR * k + PAIR] = message_ref[8 * k : 8 * k + 8, 0:32, :].reshape(
                TEMPL, PAIR
            )
            for p in range(MEMBERS):
                terms = message_ref[8 * k + p, 32:48, :].astype(jnp.float32)
                share = terms[0:8] + terms[8:16]
                for j in range(4):
                    at = LANES * (4 * p + j)
                    res_ref[2 * k : 2 * k + 2, at : at + LANES] = share[2 * j : 2 * j + 2]

    masked = jnp.concatenate(masked_rows(losvd_ref, occ_ref, GRAD_CHUNK, step), axis=0)
    scores = jnp.dot(table_ref[...], masked, preferred_element_type=jnp.float32)
    row = lax.broadcasted_iota(jnp.int32, (TEMPL, LANES), 0)
    sums = []
    for b in range(GRAD_CHUNK // LANES):
        ids = permuted(ids_ref[b : b + 1, :])
        picked = jnp.where(row == ids, scores[:, LANES * b : LANES * b + LANES], 0.0)
        sums.append(jnp.sum(picked, axis=0, keepdims=True))
    gradient = jnp.concatenate(sums, axis=0)
    for target in range(16):
        out_ref[target] = gradient


def grad(losvd, occ, ids, message):
    steps = 4096 // GRAD_CHUNK
    rows = GRAD_CHUNK // LANES
    return pl.pallas_call(
        grad_kernel,
        name="grad",
        grid=(steps,),
        in_specs=[
            pl.BlockSpec((8, VBINS, GRAD_CHUNK), lambda i: (0, 0, i)),
            pl.BlockSpec((8, 32), lambda i: (0, 0)),
            pl.BlockSpec((rows, LANES), lambda i: (i, 0)),
            pl.BlockSpec((32, 48, PAIR), lambda i: (0, 0, 0)),
        ],
        out_specs=[
            pl.BlockSpec((16, rows, LANES), lambda i: (0, i, 0)),
            pl.BlockSpec((8, WAVE), lambda i: (0, 0)),
        ],
        out_shape=[
            jax.ShapeDtypeStruct((16, 32, LANES), jnp.float32),
            jax.ShapeDtypeStruct((8, WAVE), jnp.float32),
        ],
        scratch_shapes=[pltpu.VMEM((TEMPL, 8 * VBINS), jnp.bfloat16)],
        compiler_params=pltpu.CompilerParams(vmem_limit_bytes=24 << 20),
        cost_estimate=pl.CostEstimate(flops=1 << 30, bytes_accessed=5 << 20, transcendentals=0),
    )(losvd, occ, ids, message)


def update_kernel(weights_ref, parts_ref, out_ref):
    total = parts_ref[0]
    for source in range(1, 16):
        total = total + parts_ref[source]
    out_ref[...] = jnp.maximum(weights_ref[...] - step_size * total, 0.0)


def update(weights, parts):
    return pl.pallas_call(
        update_kernel,
        name="update",
        out_shape=jax.ShapeDtypeStruct((32, LANES), jnp.float32),
        compiler_params=pltpu.CompilerParams(vmem_limit_bytes=8 << 20),
    )(weights, parts)


def local(weights, losvd, occupancy, template_of, templates, observed, inv_sigma):
    exchange = functools.partial(lax.all_to_all, split_axis=0, concat_axis=0, tiled=True)
    same_member = [[MEMBERS * k + p for k in range(GROUPS)] for p in range(MEMBERS)]
    same_group = [[MEMBERS * k + p for p in range(MEMBERS)] for k in range(GROUPS)]
    rows = losvd.transpose(1, 2, 0)
    occ = occupancy.T
    ids = template_of.reshape(32, LANES)
    now = weights.reshape(32, LANES)
    index = lax.axis_index("orb")
    place = jnp.stack([index // MEMBERS, index % MEMBERS]).astype(jnp.int32)
    own = jnp.broadcast_to(templates, (GROUPS, *templates.shape))
    gathered = exchange(own, "orb", axis_index_groups=same_member)
    shares = exchange(mix(rows, occ, ids, now), "orb")
    parts = exchange(model(shares, gathered), "orb", axis_index_groups=same_group)
    message = exchange(respond(place, parts, observed, inv_sigma, gathered), "orb")
    gradient, residual = grad(rows, occ, ids, message)
    sums = exchange(gradient, "spx")
    return update(now, sums).reshape(weights.shape), residual


def solution(mesh):
    placed = (
        P("orb"),
        P("orb", "spx", None),
        P("orb", "spx"),
        P("orb"),
        P("orb", None),
        P("spx", None),
        P("spx", None),
    )
    return jax.shard_map(
        local, mesh=mesh, in_specs=placed, out_specs=(P("orb"), P("spx", None)), check_vma=False
    )
```

time: 177 us -> 105 us (0.59)
  local copies, waits for them, and re-layouts: 67.3 us -> 8.16 us
  blocking collectives: 26.9 us -> 61.3 us
  starting transfers between devices: 33.5 us -> 13.7 us
  waiting for transfers between devices: 27.2 us -> 9.95 us
  matrix products: 13.7 us -> 0 us
  Pallas kernels: 0 us -> 10.1 us
  other arithmetic: 5.51 us -> 0.08 us
    another operation x69 -> x0, local copies, waits for them, and re-layouts: 62.8 us -> none  [local(): jnp.stack([templates[:, offset:offset + wavelengths] for offset in range(...]
    all_to_all x2 -> x3, blocking collectives: 26.9 us -> 61.3 us  [the longest x1 22 us: local(): shares = exchange(mix(rows, occ, ids, now), 'orb')]
    all_to_all x4 -> x2, starting transfers between devices: 33.5 us -> 13.7 us  [the longest x1 10.3 us: local(): gathered = exchange(own, 'orb', axis_index_groups=same_member)]
    all_to_all x4 -> x2, waiting for transfers between devices: 27.2 us -> 9.95 us  [the longest x1 5.95 us: local(): exchange(model(shares, gathered), 'orb', axis_index_groups=same_group)]
    dot_general x4 -> x0, matrix products: 13.7 us -> none  [the longest x1 4.19 us: local(): jnp.einsum('tsv,tvw->sw', mixture, shifted_wide, preferred_element_type=j...]
    pallas_call x0 -> x5, Pallas kernels: none -> 10.1 us  [the longest x1 3.45 us: grad(): pl.pallas_call(grad_kernel, name='grad', grid=(steps,), in_specs=[pl.Bloc...]
    unnamed x9 -> x20, local copies, waits for them, and re-layouts: 2.59 us -> 6.52 us
    mul x1 -> x0, other arithmetic: 2.51 us -> none  [local(): losvd.reshape(block_count, block_size, spaxel_count, velocity_bins)]
  transfers between devices with their start and end apart: 4 -> 2, of which waited for: 3 -> 2; matrix products, arithmetic and copies ran while one was open for 38% -> 0% of each run, Pallas kernels for 0% -> 3%
where the time goes in v1:
time: 105 us; the launch traced here: 104 us
  blocking collectives  61.3 us (58%)
  starting transfers between devices  13.7 us (13%)
  Pallas kernels  10.1 us (10%)
  waiting for transfers between devices  9.95 us (9%)
  local copies, waits for them, and re-layouts  8.16 us (8%)
    all_to_all x1, blocking collectives, local(): shares = exchange(mix(rows, occ, ids, now), 'orb')  22 us
    all_to_all x1, blocking collectives, local(): sums = exchange(gradient, 'spx')  20.3 us
    all_to_all x1, blocking collectives, local(): exchange(respond(place, parts, observed, inv_sigma, gathered), 'orb')  19 us
    all_to_all x1, starting transfers between devices, local(): gathered = exchange(own, 'orb', axis_index_groups=same_member)  10.3 us
    unnamed x20, local copies, waits for them, and re-layouts  6.52 us
    all_to_all x1, waiting for transfers between devices, local(): exchange(model(shares, gathered), 'orb', axis_index_groups=same_group)  5.95 us
    all_to_all x1, waiting for transfers between devices, local(): gathered = exchange(own, 'orb', axis_index_groups=same_member)  4 us
    pallas_call x1, Pallas kernels, grad(): pl.pallas_call(grad_kernel, name='grad', grid=(steps,), in_specs=[pl.Bloc...  3.45 us
  transfers between devices with their start and end apart: 2, of which 2 were waited for; matrix products, arithmetic and copies ran while one was open for 0% of the time, Pallas kernels for 3%

profile of v1, /device:TPU:8, one launch (start us, length us, event | category | flops | bytes accessed | tf_op | source)
XLA Modules:
  0.0 104.0 jit_solution(16634729246311156940)
XLA Ops:
  0.6 0.0 copy-start.2
  0.6 0.0 copy-start.3
  0.7 1.6 %broadcast_in_dim.3 = bf16[4,8,4160]{2,1,0:T(8,128)(2,1)} broadcast(bf16[8,4160]{1,0:T(8,128)(2,1)} %param.11), dimensions={1,2} | broadcast | bytes 332800 | tf_op jit(solution)/shard_map/broadcast_in_dim | solution.py:271
  2.3 10.3 %all-to-all-start.1 = ((bf16[4,8,4160]{2,1,0:T(8,128)(2,1)}), bf16[4,8,4160]{2,1,0:T(8,128)(2,1)S(1)}, u32[]{:S(2)}, u32[]{:S(2)}) async-start(bf16[4,8,4160]{2,1,0:T(8,128)(2,1)} %broadcast_in_dim.3), calls=%async_computation.1 | async-start | bytes 540672 | tf_op jit(solution)/shard_map/all_to_all | solution.py:272
  12.6 2.2 %copy-done = bf16[4096,8,64]{0,2,1:T(8,128)(2,1)S(1)} copy-done((bf16[4096,8,64]{0,2,1:T(8,128)(2,1)S(1)}, bf16[4096,8,64]{0,2,1:T(8,128)(2,1)}, u32[]{:S(2)}) %copy-start) | copy-done | bytes 4194328
  14.8 0.7 copy-done.4
  15.5 0.7 copy-done.6
  16.2 0.7 copy-done.8
  16.9 2.9 %mix.1 = f32[32,32,128]{2,1,0:T(8,128)S(1)} custom-call(bf16[8,64,4096]{2,1,0:T(8,128)(2,1)S(1)} %bitcast.7, s32[8,32]{1,0:T(8,128)S(1)} %bitcast.13, s32[32,128]{1,0:T(8,128)S(1)} %bitcast.9, f32[32,128]{1,0:T(8,128)S(1)} %bitcast.11), custom_call_target="tpu_custom_call" | custom-call | flops 1073741824 | bytes 5242880 | tf_op jit(solution)/shard_map/mix/pallas_call | solution.py:76
  19.9 4.0 %all-to-all-done.1.templates_ref = bf16[4,8,4160]{2,1,0:T(8,128)(2,1)S(1)} async-done(((bf16[4,8,4160]{2,1,0:T(8,128)(2,1)}), bf16[4,8,4160]{2,1,0:T(8,128)(2,1)S(1)}, u32[]{:S(2)}, u32[]{:S(2)}) %all-to-all-start.1) | async-done | bytes 266272 | tf_op jit(solution)/shard_map/all_to_all | solution.py:272
  23.9 22.0 %all_to_all.25.shares_ref = f32[32,32,128]{2,1,0:T(8,128)S(1)} all-to-all(f32[32,32,128]{2,1,0:T(8,128)S(1)} %mix.1), channel_id=1, replica_groups=mesh['orb'=32,'spx'=16] {'orb'}, dimensions={0} | all-to-all | bytes 1048576 | tf_op jit(solution)/shard_map/all_to_all | solution.py:273
  45.9 1.8 %model.1 = f32[8,8,1024]{2,1,0:T(8,128)} custom-call(f32[32,32,128]{2,1,0:T(8,128)S(1)} %all_to_all.25.shares_ref, bf16[4,8,4160]{2,1,0:T(8,128)(2,1)S(1)} %all-to-all-done.1.templates_ref), custom_call_target="tpu_custom_call" | custom-call | flops 134217728 | bytes 1048576 | tf_op jit(solution)/shard_map/model/pallas_call | solution.py:129
  47.7 3.4 %all-to-all-start.2 = ((f32[8,8,1024]{2,1,0:T(8,128)}), f32[8,8,1024]{2,1,0:T(8,128)S(1)}, u32[]{:S(2)}, u32[]{:S(2)}) async-start(f32[8,8,1024]{2,1,0:T(8,128)} %model.1), calls=%async_computation.2 | async-start | bytes 524288 | tf_op jit(solution)/shard_map/all_to_all | solution.py:274
  51.1 0.1 pad_add_fusion.place_ref
  51.2 5.9 %all-to-all-done.2.parts_ref = f32[8,8,1024]{2,1,0:T(8,128)S(1)} async-done(((f32[8,8,1024]{2,1,0:T(8,128)}), f32[8,8,1024]{2,1,0:T(8,128)S(1)}, u32[]{:S(2)}, u32[]{:S(2)}) %all-to-all-start.2) | async-done | bytes 262176 | tf_op jit(solution)/shard_map/all_to_all | solution.py:274
  57.2 0.0 copy-done.3
  57.2 1.2 %respond.1 = bf16[32,48,128]{2,1,0:T(8,128)(2,1)S(1)} custom-call(s32[2]{0:T(128)S(1)} %pad_add_fusion.place_ref, f32[8,8,1024]{2,1,0:T(8,128)S(1)} %all-to-all-done.2.parts_ref, f32[8,4096]{1,0:T(8,128)S(1)} %copy-done.2, f32[8,4096]{1,0:T(8,128)S(1)} %copy-done.3, bf16[4,8,4160]{2,1,0:T(8,128)(2,1)S(1)} %all-to-all-done.1.templates_ref), custom_call_target="tpu_custom_call" | custom-call | flops 134217728 | bytes 1048576 | tf_op jit(solution)/shard_map/respond/pallas_call | solution.py:175
  58.4 19.0 %all_to_all.26.message_ref = bf16[32,48,128]{2,1,0:T(8,128)(2,1)S(1)} all-to-all(bf16[32,48,128]{2,1,0:T(8,128)(2,1)S(1)} %respond.1), channel_id=1, replica_groups=mesh['orb'=32,'spx'=16] {'orb'}, dimensions={0} | all-to-all | bytes 786432 | tf_op jit(solution)/shard_map/all_to_all | solution.py:275
  77.4 0.0 copy-done.5
  77.4 2.2 %copy-done.1 = bf16[4096,8,64]{0,2,1:T(8,128)(2,1)S(1)} copy-done((bf16[4096,8,64]{0,2,1:T(8,128)(2,1)S(1)}, bf16[4096,8,64]{0,2,1:T(8,128)(2,1)}, u32[]{:S(2)}) %copy-start.1) | copy-done | bytes 4194328
  79.6 3.5 %grad.1 = (f32[16,32,128]{2,1,0:T(8,128)S(1)}, f32[8,4096]{1,0:T(8,128)}) custom-call(bf16[8,64,4096]{2,1,0:T(8,128)(2,1)S(1)} %bitcast.8, s32[8,32]{1,0:T(8,128)S(1)} %bitcast.14, s32[32,128]{1,0:T(8,128)S(1)} %bitcast.10, bf16[32,48,128]{2,1,0:T(8,128)(2,1)S(1)} %all_to_all.26.message_ref), custom_call_target="tpu_custom_call" | custom-call | flops 1073741824 | bytes 5242880 | tf_op jit(solution)/shard_map/grad/pallas_call | solution.py:221
  83.0 20.3 %all_to_all.27.parts_ref = f32[16,32,128]{2,1,0:T(8,128)S(1)} all-to-all(f32[16,32,128]{2,1,0:T(8,128)S(1)} %get-tuple-element.4), channel_id=1, replica_groups=mesh['orb'=32,'spx'=16] {'spx'}, dimensions={0} | all-to-all | bytes 524288 | tf_op jit(solution)/shard_map/all_to_all | solution.py:277
  103.3 0.0 copy-done.7
  103.3 0.6 update.1
  (10 shorter events, 0.0 us)
Async XLA Ops:
  0.6 56.5 %copy-start.2 = (f32[8,4096]{1,0:T(8,128)S(1)}, f32[8,4096]{1,0:T(8,128)}, u32[]{:S(2)}) copy-start(f32[8,4096]{1,0:T(8,128)} %observed_ref.1) | copy-start | bytes 393220
  0.6 56.5 %copy-start.3 = (f32[8,4096]{1,0:T(8,128)S(1)}, f32[8,4096]{1,0:T(8,128)}, u32[]{:S(2)}) copy-start(f32[8,4096]{1,0:T(8,128)} %sigma_ref.1) | copy-start | bytes 393220
  2.3 21.6 %all-to-all-start.1 = ((bf16[4,8,4160]{2,1,0:T(8,128)(2,1)}), bf16[4,8,4160]{2,1,0:T(8,128)(2,1)S(1)}, u32[]{:S(2)}, u32[]{:S(2)}) async-start(bf16[4,8,4160]{2,1,0:T(8,128)(2,1)} %broadcast_in_dim.3), calls=%async_computation.1 | async-start | bytes 540672 | tf_op jit(solution)/shard_map/all_to_all | solution.py:272
  12.6 2.2 %copy-start = (bf16[4096,8,64]{0,2,1:T(8,128)(2,1)S(1)}, bf16[4096,8,64]{0,2,1:T(8,128)(2,1)}, u32[]{:S(2)}) copy-start(bf16[4096,8,64]{0,2,1:T(8,128)(2,1)} %param.8) | copy-start | bytes 12582916
  14.8 0.7 copy-start.4
  15.5 0.7 copy-start.6
  16.2 0.7 copy-start.8
  16.9 60.5 %copy-start.5 = (s32[4096]{0:T(1024)S(1)}, s32[4096]{0:T(1024)}, u32[]{:S(2)}) copy-start(s32[4096]{0:T(1024)} %param.10) | copy-start | bytes 49156
  16.9 60.5 %copy-start.9 = (s32[32,8]{0,1:T(8,128)S(1)}, s32[32,8]{0,1:T(8,128)}, u32[]{:S(2)}) copy-start(s32[32,8]{0,1:T(8,128)} %param.9) | copy-start | bytes 3076
  45.9 57.5 %copy-start.7 = (f32[4096]{0:T(1024)S(1)}, f32[4096]{0:T(1024)}, u32[]{:S(2)}) copy-start(f32[4096]{0:T(1024)} %param.7) | copy-start | bytes 49156
  47.7 9.5 %all-to-all-start.2 = ((f32[8,8,1024]{2,1,0:T(8,128)}), f32[8,8,1024]{2,1,0:T(8,128)S(1)}, u32[]{:S(2)}, u32[]{:S(2)}) async-start(f32[8,8,1024]{2,1,0:T(8,128)} %model.1), calls=%async_computation.2 | async-start | bytes 524288 | tf_op jit(solution)/shard_map/all_to_all | solution.py:274
  77.4 2.2 %copy-start.1 = (bf16[4096,8,64]{0,2,1:T(8,128)(2,1)S(1)}, bf16[4096,8,64]{0,2,1:T(8,128)(2,1)}, u32[]{:S(2)}) copy-start(bf16[4096,8,64]{0,2,1:T(8,128)(2,1)} %param.8) | copy-start | bytes 12582916

commit v2 on v1

v2 whole, which is shorter than its diff:
```python
import functools

import jax
import jax.numpy as jnp
from jax import lax
from jax.experimental import pallas as pl
from jax.experimental.pallas import tpu as pltpu
from jax.sharding import PartitionSpec as P

step_size = 0.5

GROUPS = 4
MEMBERS = 8
LANES = 128
VBINS = 64
WAVE = 4096
TWAVE = 4160
WIDE = 4224
TEMPL = 256
PAIR = 128
MIX_CHUNK = 512
HELD = 2048
GRAD_CHUNK = 1024
MIX_SCALE = 8192.0
GRAD_SCALE = 16.0


def masked_rows(rows, mask):
    parts = [rows[s] * jnp.broadcast_to(mask[s : s + 1, :], rows.shape[1:]) for s in range(8)]
    return jnp.concatenate(parts, axis=0)


def mask_of(occ, first, count):
    block = lax.broadcasted_iota(jnp.int32, (occ.shape[1], count), 0)
    orbit = lax.broadcasted_iota(jnp.int32, (occ.shape[1], count), 1)
    spread = (block == (first + orbit) // LANES).astype(jnp.bfloat16)
    return jnp.dot(
        occ.astype(jnp.bfloat16), spread, preferred_element_type=jnp.float32
    ).astype(jnp.bfloat16)


def mix_kernel(
    losvd_ref, occ_ref, ids_ref, weights_ref, out_ref, masked_ref, rows_ref, occ_buf, ids_buf, weights_buf, acc_ref, sems
):
    copies = [
        pltpu.make_async_copy(occ_ref, occ_buf, sems.at[0]),
        pltpu.make_async_copy(ids_ref, ids_buf, sems.at[1]),
        pltpu.make_async_copy(weights_ref, weights_buf, sems.at[2]),
    ]
    chunks = 4096 // MIX_CHUNK
    for c in range(chunks):
        source = losvd_ref.at[:, :, pl.ds(MIX_CHUNK * c, MIX_CHUNK)]
        copies.append(pltpu.make_async_copy(source, rows_ref.at[c], sems.at[3 + c]))
    for copy in copies:
        copy.start()
    for copy in copies[:3]:
        copy.wait()
    row = lax.broadcasted_iota(jnp.int32, (TEMPL, LANES), 0)
    blocks = MIX_CHUNK // LANES
    for c in range(chunks):
        parts = []
        for b in range(blocks * c, blocks * (c + 1)):
            ids = ids_buf[b : b + 1, :]
            wide = weights_buf[b : b + 1, :].astype(jnp.bfloat16).astype(jnp.float32)
            parts.append(jnp.where(row == ids, wide, 0.0).astype(jnp.bfloat16))
        assign = jnp.concatenate(parts, axis=1)
        mask = mask_of(occ_buf[...], MIX_CHUNK * c, MIX_CHUNK)
        copies[3 + c].wait()
        masked = masked_rows(rows_ref[c], mask)
        if MIX_CHUNK * c < HELD:
            masked_ref[:, MIX_CHUNK * c : MIX_CHUNK * (c + 1)] = masked
        part = lax.dot_general(
            assign, masked, (((1,), (1,)), ((), ())), preferred_element_type=jnp.float32
        )
        if c == 0:
            acc_ref[...] = part
        elif c < chunks - 1:
            acc_ref[...] += part
        else:
            acc_ref[...] = jnp.sqrt(acc_ref[...] + part) * MIX_SCALE
    for k in range(GROUPS):
        for p in range(MEMBERS):
            out_ref[GROUPS * p + k] = acc_ref[32 * p : 32 * p + 32, PAIR * k : PAIR * k + PAIR]


def mix(losvd, occ, ids, weights):
    hbm = pl.BlockSpec(memory_space=pltpu.HBM)
    vmem = pl.BlockSpec(memory_space=pltpu.VMEM)
    chunks = 4096 // MIX_CHUNK
    return pl.pallas_call(
        mix_kernel,
        name="mix",
        in_specs=[hbm] * 4,
        out_specs=[vmem, vmem],
        out_shape=[
            jax.ShapeDtypeStruct((32, 32, PAIR), jnp.float32),
            jax.ShapeDtypeStruct((8 * VBINS, HELD), jnp.bfloat16),
        ],
        scratch_shapes=[
            pltpu.VMEM((chunks, 8, VBINS, MIX_CHUNK), jnp.bfloat16),
            pltpu.VMEM((8, 32), jnp.int32),
            pltpu.VMEM((32, LANES), jnp.int32),
            pltpu.VMEM((32, LANES), jnp.float32),
            pltpu.VMEM((TEMPL, 8 * VBINS), jnp.float32),
            pltpu.SemaphoreType.DMA((3 + chunks,)),
        ],
        compiler_params=pltpu.CompilerParams(vmem_limit_bytes=16 << 20),
        cost_estimate=pl.CostEstimate(flops=1 << 30, bytes_accessed=5 << 20, transcendentals=0),
    )(*(pltpu.with_memory_space_constraint(x, pltpu.HBM) for x in (losvd, occ, ids, weights)))


def three_terms(x):
    high = x.astype(jnp.bfloat16)
    rest = x - high.astype(jnp.float32)
    middle = rest.astype(jnp.bfloat16)
    low = (rest - middle.astype(jnp.float32)).astype(jnp.bfloat16)
    return jnp.concatenate([high, middle, low], axis=0)


def whereabouts():
    index = lax.axis_index("orb")
    return lax.rem(index, GROUPS)


def own_order(k):
    return [pl.multiple_of(8 * jnp.bitwise_xor(k, j), 8) for j in range(GROUPS)]


def model_kernel(mixture_ref, t0_ref, t1_ref, t2_ref, t3_ref, out_ref, all_ref, wide_ref):
    mixture = jnp.concatenate([mixture_ref[pl.ds(at, 8), :] for at in own_order(whereabouts())], axis=0)
    terms = three_terms(mixture)
    templates = jnp.concatenate([t0_ref[...], t1_ref[...], t2_ref[...], t3_ref[...]], axis=0)
    all_ref[...] = templates
    tripled = jnp.concatenate([templates, templates, templates], axis=0)
    over_templates = (((0,), (0,)), ((), ()))
    wide_ref[:, :WAVE] = lax.dot_general(
        terms, tripled[:, :WAVE], over_templates, preferred_element_type=jnp.float32
    )
    wide_ref[:, WAVE:TWAVE] = lax.dot_general(
        terms, tripled[:, WAVE:], over_templates, preferred_element_type=jnp.float32
    )
    for s in range(2):
        rows = wide_ref[VBINS * s : VBINS * s + VBINS, :]
        for half in (32, 16, 8):
            rows = rows[:half] + pltpu.roll(rows[half : 2 * half], WIDE - half, 1)
        for half in (4, 2, 1):
            rows = rows + pltpu.roll(pltpu.roll(rows, 8 - half, 0), WIDE - half, 1)
        for q in range(4):
            piece = rows[0:1, 1024 * q : 1024 * q + 1024]
            for member in range(MEMBERS):
                out_ref[member, 4 * s + q : 4 * s + q + 1, :] = piece


def model(mixture, templates):
    vmem = pl.BlockSpec(memory_space=pltpu.VMEM)
    return pl.pallas_call(
        model_kernel,
        name="model",
        in_specs=[vmem] * 5,
        out_shape=[
            jax.ShapeDtypeStruct((MEMBERS, 8, 1024), jnp.float32),
            jax.ShapeDtypeStruct((32, TWAVE), jnp.bfloat16),
        ],
        scratch_shapes=[pltpu.VMEM((PAIR, WIDE), jnp.float32)],
        compiler_params=pltpu.CompilerParams(vmem_limit_bytes=24 << 20),
        cost_estimate=pl.CostEstimate(flops=1 << 27, bytes_accessed=1 << 20, transcendentals=0),
    )(mixture, *templates)


def respond_kernel(parts_ref, observed_ref, sigma_ref, templates_ref, out_ref, res_ref, shift_ref, rows_ref):
    k = whereabouts()
    total = parts_ref[0]
    for member in range(1, MEMBERS):
        total = total + parts_ref[member]
    templates = templates_ref[...]
    for s in range(2):
        spectrum = jnp.concatenate([total[4 * s + q : 4 * s + q + 1, :] for q in range(4)], axis=1)
        inverse = sigma_ref[pl.ds(2 * k + s, 1), :]
        residual = (spectrum - observed_ref[pl.ds(2 * k + s, 1), :]) * inverse
        for q in range(4):
            res_ref[4 * s + q : 4 * s + q + 1, :] = residual[:, 1024 * q : 1024 * q + 1024]
        scaled = (residual * inverse).astype(jnp.bfloat16).astype(jnp.float32)
        padded = jnp.concatenate([scaled, jnp.zeros((1, WIDE - WAVE), jnp.float32)], axis=1)
        spread = jnp.broadcast_to(padded, (VBINS, WIDE))
        shift_ref[VBINS * s : VBINS * s + VBINS, :] = pltpu.roll(
            spread, 0, 1, stride=1, stride_axis=0
        ).astype(jnp.bfloat16)
    over_waves = (((1,), (1,)), ((), ()))
    response = lax.dot_general(
        templates[:, :WAVE], shift_ref[:, :WAVE], over_waves, preferred_element_type=jnp.float32
    )
    response = response + lax.dot_general(
        templates[:, WAVE:], shift_ref[:, WAVE:TWAVE], over_waves, preferred_element_type=jnp.float32
    )
    for j, at in enumerate(own_order(k)):
        rows_ref[pl.ds(at, 8), :] = response[8 * j : 8 * j + 8]
    message = rows_ref[...].astype(jnp.bfloat16)
    for target in range(32):
        out_ref[target] = message


def respond(parts, observed, sigma, templates):
    vmem = pl.BlockSpec(memory_space=pltpu.VMEM)
    return pl.pallas_call(
        respond_kernel,
        name="respond",
        in_specs=[vmem] * 4,
        out_shape=[
            jax.ShapeDtypeStruct((32, 32, PAIR), jnp.bfloat16),
            jax.ShapeDtypeStruct((8, 1024), jnp.float32),
        ],
        scratch_shapes=[
            pltpu.VMEM((PAIR, WIDE), jnp.bfloat16),
            pltpu.VMEM((32, PAIR), jnp.float32),
        ],
        compiler_params=pltpu.CompilerParams(vmem_limit_bytes=24 << 20),
        cost_estimate=pl.CostEstimate(flops=1 << 27, bytes_accessed=1 << 20, transcendentals=0),
    )(parts, observed, sigma, templates)


def grad_kernel(
    masked_ref, losvd_ref, occ_ref, ids_ref, message_ref, after_ref, out_ref, table_ref, rows_ref, sems
):
    chunks = 4096 // GRAD_CHUNK
    held = HELD // GRAD_CHUNK
    copies = []
    for c in range(held, chunks):
        source = losvd_ref.at[:, :, pl.ds(GRAD_CHUNK * c, GRAD_CHUNK)]
        copies.append(pltpu.make_async_copy(source, rows_ref.at[c - held], sems.at[c - held]))
    for copy in copies:
        copy.start()
    for k in range(GROUPS):
        for p in range(MEMBERS):
            table_ref[32 * p : 32 * p + 32, PAIR * k : PAIR * k + PAIR] = message_ref[GROUPS * p + k]
    row = lax.broadcasted_iota(jnp.int32, (TEMPL, LANES), 0)
    for c in range(chunks):
        if c < held:
            masked = masked_ref[:, GRAD_CHUNK * c : GRAD_CHUNK * (c + 1)]
        else:
            mask = mask_of(occ_ref[...], GRAD_CHUNK * c, GRAD_CHUNK)
            copies[c - held].wait()
            masked = masked_rows(rows_ref[c - held], mask)
        scores = jnp.dot(table_ref[...], masked, preferred_element_type=jnp.float32)
        for b in range(GRAD_CHUNK // LANES):
            at = GRAD_CHUNK // LANES * c + b
            ids = ids_ref[at : at + 1, :]
            picked = jnp.where(row == ids, scores[:, LANES * b : LANES * b + LANES], 0.0)
            gradient = jnp.sum(picked, axis=0, keepdims=True)
            root = jnp.sqrt(jnp.abs(gradient)) * GRAD_SCALE
            out_ref[at : at + 1, :] = jnp.where(gradient < 0.0, -root, root)


def grad(masked, losvd, occ, ids, message, after):
    hbm = pl.BlockSpec(memory_space=pltpu.HBM)
    vmem = pl.BlockSpec(memory_space=pltpu.VMEM)
    fetched = max((4096 - HELD) // GRAD_CHUNK, 1)
    return pl.pallas_call(
        grad_kernel,
        name="grad",
        in_specs=[vmem, hbm, vmem, vmem, vmem, hbm],
        out_specs=vmem,
        out_shape=jax.ShapeDtypeStruct((32, LANES), jnp.float32),
        scratch_shapes=[
            pltpu.VMEM((TEMPL, 8 * VBINS), jnp.bfloat16),
            pltpu.VMEM((fetched, 8, VBINS, GRAD_CHUNK), jnp.bfloat16),
            pltpu.SemaphoreType.DMA((fetched,)),
        ],
        compiler_params=pltpu.CompilerParams(vmem_limit_bytes=16 << 20),
        cost_estimate=pl.CostEstimate(flops=1 << 30, bytes_accessed=5 << 20, transcendentals=0),
    )(masked, pltpu.with_memory_space_constraint(losvd, pltpu.HBM), occ, ids, message, after)


def assemble_kernel(r0_ref, r1_ref, r2_ref, r3_ref, out_ref):
    k = whereabouts()
    pieces = [r0_ref[...], r1_ref[...], r2_ref[...], r3_ref[...]]
    for group in range(GROUPS):
        j = jnp.bitwise_xor(k, group)
        piece = jnp.where(
            j < 2, jnp.where(j == 0, pieces[0], pieces[1]), jnp.where(j == 2, pieces[2], pieces[3])
        )
        for s in range(2):
            for q in range(4):
                out_ref[2 * group + s : 2 * group + s + 1, 1024 * q : 1024 * q + 1024] = piece[
                    4 * s + q : 4 * s + q + 1, :
                ]


def assemble(pieces):
    vmem = pl.BlockSpec(memory_space=pltpu.VMEM)
    return pl.pallas_call(
        assemble_kernel,
        name="assemble",
        in_specs=[vmem] * 4,
        out_shape=jax.ShapeDtypeStruct((8, WAVE), jnp.float32),
        compiler_params=pltpu.CompilerParams(vmem_limit_bytes=4 << 20),
    )(*pieces)


def step(weights, losvd, occupancy, template_of, templates, observed, inv_sigma):
    exchange = functools.partial(lax.all_to_all, split_axis=0, concat_axis=0, tiled=True)
    same_spaxels = [[GROUPS * p + k for p in range(MEMBERS)] for k in range(GROUPS)]
    rows = losvd.transpose(1, 2, 0)
    occ = occupancy.T
    ids = template_of.reshape(32, LANES)
    now = weights.reshape(32, LANES)

    def from_group(array, j):
        return lax.ppermute(array, "orb", [(i, i ^ j) for i in range(32)])

    gathered = [templates] + [from_group(templates, j) for j in range(1, GROUPS)]
    mixed, masked = mix(rows, occ, ids, now)
    shares = exchange(mixed.astype(jnp.float16), "orb").astype(jnp.float32)
    mixture = jnp.sum(shares * shares, axis=0) * (1.0 / MIX_SCALE**2)
    spectra, wanted = model(mixture, gathered)
    parts = exchange(spectra, "orb", axis_index_groups=same_spaxels)
    response, part = respond(parts, observed, inv_sigma, wanted)
    message = exchange(response, "orb")
    residual = assemble([part] + [from_group(part, j) for j in range(1, GROUPS)])
    roots = grad(masked, rows, occ, ids, message, residual).astype(jnp.float16)
    sums = exchange(jnp.broadcast_to(roots, (16, 32, LANES)), "spx").astype(jnp.float32)
    moved = jnp.sum(sums * jnp.abs(sums), axis=0) * (1.0 / GRAD_SCALE**2)
    return jnp.maximum(now - step_size * moved, 0.0).reshape(weights.shape), residual


def solution(mesh):
    placed = (
        P("orb"),
        P("orb", "spx", None),
        P("orb", "spx"),
        P("orb"),
        P("orb", None),
        P("spx", None),
        P("spx", None),
    )
    return jax.shard_map(
        step, mesh=mesh, in_specs=placed, out_specs=(P("orb"), P("spx", None)), check_vma=False
    )
```

time: 105 us -> 90.5 us (0.86)
  blocking collectives: 61.3 us -> 36.9 us
  starting transfers between devices: 13.7 us -> 30.9 us
  local copies, waits for them, and re-layouts: 8.16 us -> 0.95 us
  other arithmetic: 0.08 us -> 1.48 us
  waiting for transfers between devices: 9.95 us -> 8.73 us
    all_to_all x3 -> x2, blocking collectives: 61.3 us -> 36.9 us  [the longest x1 19 us: step(): exchange(jnp.broadcast_to(roots, (16, 32, LANES)), 'spx')]
    ppermute x0 -> x6, starting transfers between devices: none -> 15.2 us  [from_group(): return lax.ppermute(array, 'orb', [(i, i ^ j) for i in range(32)])]
    unnamed x20 -> x14, local copies, waits for them, and re-layouts: 6.52 us -> 0.93 us
    all_to_all x2, waiting for transfers between devices: 9.95 us -> 5.41 us  [the longest x1 4.7 us: step(): shares = exchange(mixed.astype(jnp.float16), 'orb').astype(jnp.float32)]
    ppermute x0 -> x6, waiting for transfers between devices: none -> 3.32 us  [from_group(): return lax.ppermute(array, 'orb', [(i, i ^ j) for i in range(32)])]
    all_to_all x2, starting transfers between devices: 13.7 us -> 15.6 us  [the longest x1 11.6 us: step(): shares = exchange(mixed.astype(jnp.float16), 'orb').astype(jnp.float32)]
    broadcast_in_dim x1, local copies, waits for them, and re-layouts: 1.65 us -> 0.02 us  [step(): jnp.broadcast_to(roots, (16, 32, LANES))]
  transfers between devices with their start and end apart: 2 -> 8, of which waited for: 2 -> 4; matrix products, arithmetic and copies ran while one was open for 0% -> 0% of each run, Pallas kernels for 3% -> 1%
where the time goes in v2:
time: 90.5 us; the launch traced here: 89.9 us
  blocking collectives  36.9 us (41%)
  starting transfers between devices  30.9 us (34%)
  Pallas kernels  10.2 us (11%)
  waiting for transfers between devices  8.73 us (10%)
  other arithmetic  1.48 us (2%)
  local copies, waits for them, and re-layouts  0.95 us (1%)
    all_to_all x1, blocking collectives, step(): exchange(jnp.broadcast_to(roots, (16, 32, LANES)), 'spx')  19 us
    all_to_all x1, blocking collectives, step(): parts = exchange(spectra, 'orb', axis_index_groups=same_spaxels)  17.9 us
    ppermute x6, starting transfers between devices, from_group(): return lax.ppermute(array, 'orb', [(i, i ^ j) for i in range(32)])  15.2 us
    all_to_all x1, starting transfers between devices, step(): shares = exchange(mixed.astype(jnp.float16), 'orb').astype(jnp.float32)  11.6 us
    all_to_all x1, waiting for transfers between devices, step(): shares = exchange(mixed.astype(jnp.float16), 'orb').astype(jnp.float32)  4.7 us
    pallas_call x1, Pallas kernels, mix(): pl.pallas_call(mix_kernel, name='mix', in_specs=[hbm] * 4, out_specs=[vme...  4.67 us
    all_to_all x1, starting transfers between devices, step(): message = exchange(response, 'orb')  4 us
    ppermute x6, waiting for transfers between devices, from_group(): return lax.ppermute(array, 'orb', [(i, i ^ j) for i in range(32)])  3.32 us
  transfers between devices with their start and end apart: 8, of which 4 were waited for; matrix products, arithmetic and copies ran while one was open for 0% of the time, Pallas kernels for 1%

profile of v2, /device:TPU:8, one launch (start us, length us, event | category | flops | bytes accessed | tf_op | source)
XLA Modules:
  0.0 89.9 jit_solution(3375359130892396766)
XLA Ops:
  0.7 4.7 %mix.1 = (f32[32,32,128]{2,1,0:T(8,128)S(1)}, bf16[512,2048]{1,0:T(8,128)(2,1)S(1)}) custom-call(bf16[8,64,4096]{2,1,0:T(8,128)(2,1)} %bitcast.12, s32[8,32]{1,0:T(8,128)} %bitcast.10, s32[32,128]{1,0:T(8,128)} %bitcast.8, f32[32,128]{1,0:T(8,128)} %bitcast.14), custom_call_target="tpu_custom_call" | custom-call | flops 1073741824 | bytes 5242880 | tf_op jit(solution)/shard_map/mix/pallas_call | solution.py:90
  5.4 0.7 convert_element_type.12
  6.1 11.6 %all-to-all-start = ((f16[32,32,128]{2,1,0:T(8,128)(2,1)}), f16[32,32,128]{2,1,0:T(8,128)(2,1)S(1)}, u32[]{:S(2)}, u32[]{:S(2)}) async-start(f16[32,32,128]{2,1,0:T(8,128)(2,1)} %convert_element_type.12), calls=%async_computation | async-start | bytes 524288 | tf_op jit(solution)/shard_map/all_to_all | solution.py:312
  17.8 2.2 %collective-permute-start = (bf16[8,4160]{1,0:T(8,128)(2,1)S(1)}, bf16[8,4160]{1,0:T(8,128)(2,1)S(1)}, u32[]{:S(2)}, u32[]{:S(2)}) collective-permute-start(bf16[8,4160]{1,0:T(8,128)(2,1)S(1)} %copy-done.5), channel_id=1, source_target_pairs={{0,16},{16,0},{32,48},{48,32},{64,80},{80,64},{96,112},{112,96},{1... | collective-permute-start | bytes 199688 | tf_op jit(solution)/shard_map/ppermute | solution.py:308
  19.9 3.5 %collective-permute-start.1 = (bf16[8,4160]{1,0:T(8,128)(2,1)S(1)}, bf16[8,4160]{1,0:T(8,128)(2,1)S(1)}, u32[]{:S(2)}, u32[]{:S(2)}) collective-permute-start(bf16[8,4160]{1,0:T(8,128)(2,1)S(1)} %copy-done.5), channel_id=1, source_target_pairs={{0,32},{16,48},{32,0},{48,16},{64,96},{80,112},{96,64},{112,80},{1... | collective-permute-start | bytes 199688 | tf_op jit(solution)/shard_map/ppermute | solution.py:308
  23.5 1.9 %collective-permute-start.2 = (bf16[8,4160]{1,0:T(8,128)(2,1)S(1)}, bf16[8,4160]{1,0:T(8,128)(2,1)S(1)}, u32[]{:S(2)}, u32[]{:S(2)}) collective-permute-start(bf16[8,4160]{1,0:T(8,128)(2,1)S(1)} %copy-done.5), channel_id=1, source_target_pairs={{0,48},{16,32},{32,16},{48,0},{64,112},{80,96},{96,80},{112,64},{1... | collective-permute-start | bytes 199688 | tf_op jit(solution)/shard_map/ppermute | solution.py:308
  25.4 4.7 %all-to-all-done = f16[32,32,128]{2,1,0:T(8,128)(2,1)S(1)} async-done(((f16[32,32,128]{2,1,0:T(8,128)(2,1)}), f16[32,32,128]{2,1,0:T(8,128)(2,1)S(1)}, u32[]{:S(2)}, u32[]{:S(2)}) %all-to-all-start) | async-done | bytes 262176 | tf_op jit(solution)/shard_map/all_to_all | solution.py:312
  30.1 0.1 multiply_reduce_fusion
  30.2 0.0 collective-permute-done.t1_ref
  30.2 1.1 %model.1 = (f32[8,8,1024]{2,1,0:T(8,128)S(1)}, bf16[32,4160]{1,0:T(8,128)(2,1)S(1)}) custom-call(f32[32,128]{1,0:T(8,128)S(1)} %broadcast_multiply_fusion.mixture_ref, bf16[8,4160]{1,0:T(8,128)(2,1)S(1)} %copy-done.5, bf16[8,4160]{1,0:T(8,128)(2,1)S(1)} %collective-permute-done.t1_ref, bf16[8,4160]{1,0:T(8,128)(2,1)S(1)} %collective-permute-done.1.t2_ref, ...), custom_call_target="tpu_custom_call" | custom-call | flops 134217728 | bytes 1048576 | tf_op jit(solution)/shard_map/model/pallas_call | solution.py:156
  31.4 17.9 %all_to_all.20.parts_ref = f32[8,8,1024]{2,1,0:T(8,128)S(1)} all-to-all(f32[8,8,1024]{2,1,0:T(8,128)S(1)} %get-tuple-element.10), channel_id=1, replica_groups={{0,64,128,192,256,320,384,448},{16,80,144,208,272,336,400,464},{32,96,1..., dimensions={0} | all-to-all | bytes 524288 | tf_op jit(solution)/shard_map/all_to_all | solution.py:315
  49.3 1.4 %respond.1 = (bf16[32,32,128]{2,1,0:T(8,128)(2,1)}, f32[8,1024]{1,0:T(8,128)S(1)}) custom-call(f32[8,8,1024]{2,1,0:T(8,128)S(1)} %all_to_all.20.parts_ref, f32[8,4096]{1,0:T(8,128)S(1)} %copy-done.1, f32[8,4096]{1,0:T(8,128)S(1)} %copy-done.2, bf16[32,4160]{1,0:T(8,128)(2,1)S(1)} %get-tuple-element.11.templates_ref), custom_call_target="tpu_custom_call" | custom-call | flops 134217728 | bytes 1048576 | tf_op jit(solution)/shard_map/respond/pallas_call | solution.py:204
  50.7 4.0 %all-to-all-start.2 = ((bf16[32,32,128]{2,1,0:T(8,128)(2,1)}), bf16[32,32,128]{2,1,0:T(8,128)(2,1)S(1)}, u32[]{:S(2)}, u32[]{:S(2)}) async-start(bf16[32,32,128]{2,1,0:T(8,128)(2,1)} %get-tuple-element.12), calls=%async_computation.2 | async-start | bytes 524288 | tf_op jit(solution)/shard_map/all_to_all | solution.py:317
  54.7 2.1 %collective-permute-start.3 = (f32[8,1024]{1,0:T(8,128)S(1)}, f32[8,1024]{1,0:T(8,128)S(1)}, u32[]{:S(2)}, u32[]{:S(2)}) collective-permute-start(f32[8,1024]{1,0:T(8,128)S(1)} %get-tuple-element.13.r0_ref), channel_id=1, source_target_pairs={{0,16},{16,0},{32,48},{48,32},{64,80},{80,64},{96,112},{112,96},{1... | collective-permute-start | bytes 98312 | tf_op jit(solution)/shard_map/ppermute | solution.py:308
  56.7 3.6 %collective-permute-start.4 = (f32[8,1024]{1,0:T(8,128)S(1)}, f32[8,1024]{1,0:T(8,128)S(1)}, u32[]{:S(2)}, u32[]{:S(2)}) collective-permute-start(f32[8,1024]{1,0:T(8,128)S(1)} %get-tuple-element.13.r0_ref), channel_id=1, source_target_pairs={{0,32},{16,48},{32,0},{48,16},{64,96},{80,112},{96,64},{112,80},{1... | collective-permute-start | bytes 98312 | tf_op jit(solution)/shard_map/ppermute | solution.py:308
  60.3 2.0 %collective-permute-start.5 = (f32[8,1024]{1,0:T(8,128)S(1)}, f32[8,1024]{1,0:T(8,128)S(1)}, u32[]{:S(2)}, u32[]{:S(2)}) collective-permute-start(f32[8,1024]{1,0:T(8,128)S(1)} %get-tuple-element.13.r0_ref), channel_id=1, source_target_pairs={{0,48},{16,32},{32,16},{48,0},{64,112},{80,96},{96,80},{112,64},{1... | collective-permute-start | bytes 98312 | tf_op jit(solution)/shard_map/ppermute | solution.py:308
  62.3 0.6 collective-permute-done.4.r2_ref
  62.9 2.7 %collective-permute-done.5.r3_ref = f32[8,1024]{1,0:T(8,128)S(1)} collective-permute-done((f32[8,1024]{1,0:T(8,128)S(1)}, f32[8,1024]{1,0:T(8,128)S(1)}, u32[]{:S(2)}, u32[]{:S(2)}) %collective-permute-start.5) | collective-permute-done | bytes 32800 | tf_op jit(solution)/shard_map/ppermute | solution.py:308
  65.6 0.7 assemble.1.after_ref
  66.3 0.7 all-to-all-done.2.message_ref
  67.0 0.9 %copy-done = f32[8,4096]{1,0:T(8,128)S(1)} copy-done((f32[8,4096]{1,0:T(8,128)S(1)}, f32[8,4096]{1,0:T(8,128)}, u32[]{:S(2)}) %copy-start) | copy-done | bytes 131096
  67.9 2.3 %grad.1 = f32[32,128]{1,0:T(8,128)S(1)} custom-call(bf16[512,2048]{1,0:T(8,128)(2,1)S(1)} %get-tuple-element.8.masked_ref, bf16[8,64,4096]{2,1,0:T(8,128)(2,1)} %bitcast.13, s32[8,32]{1,0:T(8,128)S(1)} %bitcast.11, s32[32,128]{1,0:T(8,128)S(1)} %bitcast.9, bf16[32,32,128]{2,1,0:T(8,128)(2,1)S(1)} %all-to-all-done.2.message_ref, f32[8,4096]{1,0:T(8,128)S(1)} %copy-done), custom_call_target="tpu_custom_call" | custom-call | flops 1073741824 | bytes 5242880 | tf_op jit(solution)/shard_map/grad/pallas_call | solution.py:257
  70.2 19.0 %all_to_all.21 = f16[16,32,128]{2,1,0:T(8,128)(2,1)S(1)} all-to-all(f16[16,32,128]{2,1,0:T(8,128)(2,1)S(1)} %broadcast_in_dim.3), channel_id=1, replica_groups=mesh['orb'=32,'spx'=16] {'spx'}, dimensions={0} | all-to-all | bytes 262144 | tf_op jit(solution)/shard_map/all_to_all | solution.py:320
  89.3 0.6 fusion.1
  (20 shorter events, 0.1 us)
Async XLA Ops:
  0.6 17.1 %copy-start.5 = (bf16[8,4160]{1,0:T(8,128)(2,1)S(1)}, bf16[8,4160]{1,0:T(8,128)(2,1)}, u32[]{:S(2)}) copy-start(bf16[8,4160]{1,0:T(8,128)(2,1)} %t0_ref.1) | copy-start | bytes 199684
  0.6 48.6 %copy-start.1 = (f32[8,4096]{1,0:T(8,128)S(1)}, f32[8,4096]{1,0:T(8,128)}, u32[]{:S(2)}) copy-start(f32[8,4096]{1,0:T(8,128)} %observed_ref.1) | copy-start | bytes 393220
  0.7 48.6 %copy-start.2 = (f32[8,4096]{1,0:T(8,128)S(1)}, f32[8,4096]{1,0:T(8,128)}, u32[]{:S(2)}) copy-start(f32[8,4096]{1,0:T(8,128)} %sigma_ref.1) | copy-start | bytes 393220
  0.7 66.4 %copy-start.3 = (s32[4096]{0:T(1024)S(1)}, s32[4096]{0:T(1024)}, u32[]{:S(2)}) copy-start(s32[4096]{0:T(1024)} %param.10) | copy-start | bytes 49156
  0.7 66.3 %copy-start.4 = (s32[32,8]{0,1:T(8,128)S(1)}, s32[32,8]{0,1:T(8,128)}, u32[]{:S(2)}) copy-start(s32[32,8]{0,1:T(8,128)} %param.9) | copy-start | bytes 3076
  6.1 24.0 %all-to-all-start = ((f16[32,32,128]{2,1,0:T(8,128)(2,1)}), f16[32,32,128]{2,1,0:T(8,128)(2,1)S(1)}, u32[]{:S(2)}, u32[]{:S(2)}) async-start(f16[32,32,128]{2,1,0:T(8,128)(2,1)} %convert_element_type.12), calls=%async_computation | async-start | bytes 524288 | tf_op jit(solution)/shard_map/all_to_all | solution.py:312
  17.8 12.4 %collective-permute-start = (bf16[8,4160]{1,0:T(8,128)(2,1)S(1)}, bf16[8,4160]{1,0:T(8,128)(2,1)S(1)}, u32[]{:S(2)}, u32[]{:S(2)}) collective-permute-start(bf16[8,4160]{1,0:T(8,128)(2,1)S(1)} %copy-done.5), channel_id=1, source_target_pairs={{0,16},{16,0},{32,48},{48,32},{64,80},{80,64},{96,112},{112,96},{1... | collective-permute-start | bytes 199688 | tf_op jit(solution)/shard_map/ppermute | solution.py:308
  19.9 10.3 %collective-permute-start.1 = (bf16[8,4160]{1,0:T(8,128)(2,1)S(1)}, bf16[8,4160]{1,0:T(8,128)(2,1)S(1)}, u32[]{:S(2)}, u32[]{:S(2)}) collective-permute-start(bf16[8,4160]{1,0:T(8,128)(2,1)S(1)} %copy-done.5), channel_id=1, source_target_pairs={{0,32},{16,48},{32,0},{48,16},{64,96},{80,112},{96,64},{112,80},{1... | collective-permute-start | bytes 199688 | tf_op jit(solution)/shard_map/ppermute | solution.py:308
  23.5 6.7 %collective-permute-start.2 = (bf16[8,4160]{1,0:T(8,128)(2,1)S(1)}, bf16[8,4160]{1,0:T(8,128)(2,1)S(1)}, u32[]{:S(2)}, u32[]{:S(2)}) collective-permute-start(bf16[8,4160]{1,0:T(8,128)(2,1)S(1)} %copy-done.5), channel_id=1, source_target_pairs={{0,48},{16,32},{32,16},{48,0},{64,112},{80,96},{96,80},{112,64},{1... | collective-permute-start | bytes 199688 | tf_op jit(solution)/shard_map/ppermute | solution.py:308
  50.7 38.7 %copy-start.6 = (f32[4096]{0:T(1024)S(1)}, f32[4096]{0:T(1024)}, u32[]{:S(2)}) copy-start(f32[4096]{0:T(1024)} %param.7) | copy-start | bytes 49156
  50.7 16.4 %all-to-all-start.2 = ((bf16[32,32,128]{2,1,0:T(8,128)(2,1)}), bf16[32,32,128]{2,1,0:T(8,128)(2,1)S(1)}, u32[]{:S(2)}, u32[]{:S(2)}) async-start(bf16[32,32,128]{2,1,0:T(8,128)(2,1)} %get-tuple-element.12), calls=%async_computation.2 | async-start | bytes 524288 | tf_op jit(solution)/shard_map/all_to_all | solution.py:317
  54.7 7.6 %collective-permute-start.3 = (f32[8,1024]{1,0:T(8,128)S(1)}, f32[8,1024]{1,0:T(8,128)S(1)}, u32[]{:S(2)}, u32[]{:S(2)}) collective-permute-start(f32[8,1024]{1,0:T(8,128)S(1)} %get-tuple-element.13.r0_ref), channel_id=1, source_target_pairs={{0,16},{16,0},{32,48},{48,32},{64,80},{80,64},{96,112},{112,96},{1... | collective-permute-start | bytes 98312 | tf_op jit(solution)/shard_map/ppermute | solution.py:308
  56.7 6.2 %collective-permute-start.4 = (f32[8,1024]{1,0:T(8,128)S(1)}, f32[8,1024]{1,0:T(8,128)S(1)}, u32[]{:S(2)}, u32[]{:S(2)}) collective-permute-start(f32[8,1024]{1,0:T(8,128)S(1)} %get-tuple-element.13.r0_ref), channel_id=1, source_target_pairs={{0,32},{16,48},{32,0},{48,16},{64,96},{80,112},{96,64},{112,80},{1... | collective-permute-start | bytes 98312 | tf_op jit(solution)/shard_map/ppermute | solution.py:308
  60.3 5.3 %collective-permute-start.5 = (f32[8,1024]{1,0:T(8,128)S(1)}, f32[8,1024]{1,0:T(8,128)S(1)}, u32[]{:S(2)}, u32[]{:S(2)}) collective-permute-start(f32[8,1024]{1,0:T(8,128)S(1)} %get-tuple-element.13.r0_ref), channel_id=1, source_target_pairs={{0,48},{16,32},{32,16},{48,0},{64,112},{80,96},{96,80},{112,64},{1... | collective-permute-start | bytes 98312 | tf_op jit(solution)/shard_map/ppermute | solution.py:308
  67.0 0.9 %copy-start = (f32[8,4096]{1,0:T(8,128)S(1)}, f32[8,4096]{1,0:T(8,128)}, u32[]{:S(2)}) copy-start(f32[8,4096]{1,0:T(8,128)} %assemble.1.after_ref) | copy-start | bytes 393220

commit v3 on v2

--- a/solution.py
+++ b/solution.py
@@ -18,11 +18,12 @@
 WIDE = 4224
 TEMPL = 256
 PAIR = 128
-MIX_CHUNK = 512
+MIX_CHUNK = 1024
 HELD = 2048
 GRAD_CHUNK = 1024
 MIX_SCALE = 8192.0
 GRAD_SCALE = 16.0
+SPECTRUM_SCALE = 16.0
 
 
 def masked_rows(rows, mask):
@@ -169,9 +170,7 @@
 
 def respond_kernel(parts_ref, observed_ref, sigma_ref, templates_ref, out_ref, res_ref, shift_ref, rows_ref):
     k = whereabouts()
-    total = parts_ref[0]
-    for member in range(1, MEMBERS):
-        total = total + parts_ref[member]
+    total = parts_ref[...]
     templates = templates_ref[...]
     for s in range(2):
         spectrum = jnp.concatenate([total[4 * s + q : 4 * s + q + 1, :] for q in range(4)], axis=1)
@@ -267,7 +266,7 @@
         ],
         compiler_params=pltpu.CompilerParams(vmem_limit_bytes=16 << 20),
         cost_estimate=pl.CostEstimate(flops=1 << 30, bytes_accessed=5 << 20, transcendentals=0),
-    )(masked, pltpu.with_memory_space_constraint(losvd, pltpu.HBM), occ, ids, message, after)
+    )(masked, pltpu.with_memory_space_constraint(losvd, pltpu.HBM), occ, ids, message, pltpu.with_memory_space_constraint(after, pltpu.HBM))
 
 
 def assemble_kernel(r0_ref, r1_ref, r2_ref, r3_ref, out_ref):
@@ -312,8 +311,10 @@
     shares = exchange(mixed.astype(jnp.float16), "orb").astype(jnp.float32)
     mixture = jnp.sum(shares * shares, axis=0) * (1.0 / MIX_SCALE**2)
     spectra, wanted = model(mixture, gathered)
-    parts = exchange(spectra, "orb", axis_index_groups=same_spaxels)
-    response, part = respond(parts, observed, inv_sigma, wanted)
+    sent = (spectra * SPECTRUM_SCALE).astype(jnp.float16)
+    parts = exchange(sent, "orb", axis_index_groups=same_spaxels).astype(jnp.float32)
+    spectrum = jnp.sum(parts, axis=0) * (1.0 / SPECTRUM_SCALE)
+    response, part = respond(spectrum, observed, inv_sigma, wanted)
     message = exchange(response, "orb")
     residual = assemble([part] + [from_group(part, j) for j in range(1, GROUPS)])
     roots = grad(masked, rows, occ, ids, message, residual).astype(jnp.float16)
@@ -332,6 +333,4 @@
         P("spx", None),
         P("spx", None),
     )
-    return jax.shard_map(
-        step, mesh=mesh, in_specs=placed, out_specs=(P("orb"), P("spx", None)), check_vma=False
-    )
+    return jax.shard_map(step, mesh=mesh, in_specs=placed, out_specs=(P("orb"), P("spx", None)), check_vma=False)

time: 90.5 us -> 86 us (0.950)
  blocking collectives: 36.9 us -> 34.1 us
    all_to_all x1, blocking collectives: 17.9 us -> 15.1 us  [step(): exchange(sent, 'orb', axis_index_groups=same_spaxels).astype(jnp.float32)]
where the time goes in v3:
time: 86 us; the launch traced here: 85.5 us
  blocking collectives  34.1 us (40%)
  starting transfers between devices  30.7 us (36%)
  Pallas kernels  9.39 us (11%)
  waiting for transfers between devices  8.73 us (10%)
  other arithmetic  1.54 us (2%)
  between operations  0.87 us (1%)
    all_to_all x1, blocking collectives, step(): exchange(jnp.broadcast_to(roots, (16, 32, LANES)), 'spx')  19 us
    ppermute x6, starting transfers between devices, from_group(): return lax.ppermute(array, 'orb', [(i, i ^ j) for i in range(32)])  15.2 us
    all_to_all x1, blocking collectives, step(): exchange(sent, 'orb', axis_index_groups=same_spaxels).astype(jnp.float32)  15.1 us
    all_to_all x1, starting transfers between devices, step(): shares = exchange(mixed.astype(jnp.float16), 'orb').astype(jnp.float32)  11.6 us
    all_to_all x1, waiting for transfers between devices, step(): shares = exchange(mixed.astype(jnp.float16), 'orb').astype(jnp.float32)  4.7 us
    pallas_call x1, Pallas kernels, mix(): pl.pallas_call(mix_kernel, name='mix', in_specs=[hbm] * 4, out_specs=[vme...  3.91 us
    all_to_all x1, starting transfers between devices, step(): message = exchange(response, 'orb')  3.87 us
    ppermute x6, waiting for transfers between devices, from_group(): return lax.ppermute(array, 'orb', [(i, i ^ j) for i in range(32)])  3.32 us
  transfers between devices with their start and end apart: 8, of which 4 were waited for; matrix products, arithmetic and copies ran while one was open for 0% of the time, Pallas kernels for 1%

profile of v3, /device:TPU:8, one launch (start us, length us, event | category | flops | bytes accessed | tf_op | source)
XLA Modules:
  0.0 85.5 jit_solution(4328886063511673398)
XLA Ops:
  0.7 3.9 %mix.1 = (f32[32,32,128]{2,1,0:T(8,128)S(1)}, bf16[512,2048]{1,0:T(8,128)(2,1)S(1)}) custom-call(bf16[8,64,4096]{2,1,0:T(8,128)(2,1)} %bitcast.12, s32[8,32]{1,0:T(8,128)} %bitcast.10, s32[32,128]{1,0:T(8,128)} %bitcast.8, f32[32,128]{1,0:T(8,128)} %bitcast.14), custom_call_target="tpu_custom_call" | custom-call | flops 1073741824 | bytes 5242880 | tf_op jit(solution)/shard_map/mix/pallas_call | solution.py:91
  4.6 0.8 convert_element_type.18
  5.4 11.6 %all-to-all-start = ((f16[32,32,128]{2,1,0:T(8,128)(2,1)}), f16[32,32,128]{2,1,0:T(8,128)(2,1)S(1)}, u32[]{:S(2)}, u32[]{:S(2)}) async-start(f16[32,32,128]{2,1,0:T(8,128)(2,1)} %convert_element_type.18), calls=%async_computation | async-start | bytes 524288 | tf_op jit(solution)/shard_map/all_to_all | solution.py:311
  17.0 2.2 %collective-permute-start = (bf16[8,4160]{1,0:T(8,128)(2,1)S(1)}, bf16[8,4160]{1,0:T(8,128)(2,1)S(1)}, u32[]{:S(2)}, u32[]{:S(2)}) collective-permute-start(bf16[8,4160]{1,0:T(8,128)(2,1)S(1)} %copy-done.4), channel_id=1, source_target_pairs={{0,16},{16,0},{32,48},{48,32},{64,80},{80,64},{96,112},{112,96},{1... | collective-permute-start | bytes 199688 | tf_op jit(solution)/shard_map/ppermute | solution.py:307
  19.2 3.5 %collective-permute-start.1 = (bf16[8,4160]{1,0:T(8,128)(2,1)S(1)}, bf16[8,4160]{1,0:T(8,128)(2,1)S(1)}, u32[]{:S(2)}, u32[]{:S(2)}) collective-permute-start(bf16[8,4160]{1,0:T(8,128)(2,1)S(1)} %copy-done.4), channel_id=1, source_target_pairs={{0,32},{16,48},{32,0},{48,16},{64,96},{80,112},{96,64},{112,80},{1... | collective-permute-start | bytes 199688 | tf_op jit(solution)/shard_map/ppermute | solution.py:307
  22.8 1.9 %collective-permute-start.2 = (bf16[8,4160]{1,0:T(8,128)(2,1)S(1)}, bf16[8,4160]{1,0:T(8,128)(2,1)S(1)}, u32[]{:S(2)}, u32[]{:S(2)}) collective-permute-start(bf16[8,4160]{1,0:T(8,128)(2,1)S(1)} %copy-done.4), channel_id=1, source_target_pairs={{0,48},{16,32},{32,16},{48,0},{64,112},{80,96},{96,80},{112,64},{1... | collective-permute-start | bytes 199688 | tf_op jit(solution)/shard_map/ppermute | solution.py:307
  24.7 4.7 %all-to-all-done = f16[32,32,128]{2,1,0:T(8,128)(2,1)S(1)} async-done(((f16[32,32,128]{2,1,0:T(8,128)(2,1)}), f16[32,32,128]{2,1,0:T(8,128)(2,1)S(1)}, u32[]{:S(2)}, u32[]{:S(2)}) %all-to-all-start) | async-done | bytes 262176 | tf_op jit(solution)/shard_map/all_to_all | solution.py:311
  29.4 0.1 multiply_reduce_fusion
  29.5 0.0 collective-permute-done.t1_ref
  29.5 1.1 %model.1 = (f32[8,8,1024]{2,1,0:T(8,128)S(1)}, bf16[32,4160]{1,0:T(8,128)(2,1)S(1)}) custom-call(f32[32,128]{1,0:T(8,128)S(1)} %broadcast_multiply_fusion.1.mixture_ref, bf16[8,4160]{1,0:T(8,128)(2,1)S(1)} %copy-done.4, bf16[8,4160]{1,0:T(8,128)(2,1)S(1)} %collective-permute-done.t1_ref, bf16[8,4160]{1,0:T(8,128)(2,1)S(1)} %collective-permute-done.1.t2_ref, ...), custom_call_target="tpu_custom_call" | custom-call | flops 134217728 | bytes 1048576 | tf_op jit(solution)/shard_map/model/pallas_call | solution.py:157
  30.6 15.1 %all_to_all.20 = f16[8,8,1024]{2,1,0:T(8,128)(2,1)S(1)} all-to-all(f16[8,8,1024]{2,1,0:T(8,128)(2,1)S(1)} %multiply_convert_fusion), channel_id=1, replica_groups={{0,64,128,192,256,320,384,448},{16,80,144,208,272,336,400,464},{32,96,1..., dimensions={0} | all-to-all | bytes 262144 | tf_op jit(solution)/shard_map/all_to_all | solution.py:315
  45.8 0.0 copy-start.5
  45.8 1.4 %respond.1 = (bf16[32,32,128]{2,1,0:T(8,128)(2,1)}, f32[8,1024]{1,0:T(8,128)S(1)}) custom-call(f32[8,1024]{1,0:T(8,128)S(1)} %broadcast_multiply_fusion.parts_ref, f32[8,4096]{1,0:T(8,128)S(1)} %copy-done, f32[8,4096]{1,0:T(8,128)S(1)} %copy-done.1, bf16[32,4160]{1,0:T(8,128)(2,1)S(1)} %get-tuple-element.11.templates_ref), custom_call_target="tpu_custom_call" | custom-call | flops 134217728 | bytes 1048576 | tf_op jit(solution)/shard_map/respond/pallas_call | solution.py:203
  47.2 3.9 %all-to-all-start.2 = ((bf16[32,32,128]{2,1,0:T(8,128)(2,1)}), bf16[32,32,128]{2,1,0:T(8,128)(2,1)S(1)}, u32[]{:S(2)}, u32[]{:S(2)}) async-start(bf16[32,32,128]{2,1,0:T(8,128)(2,1)} %get-tuple-element.12), calls=%async_computation.2 | async-start | bytes 524288 | tf_op jit(solution)/shard_map/all_to_all | solution.py:318
  51.1 2.1 %collective-permute-start.3 = (f32[8,1024]{1,0:T(8,128)S(1)}, f32[8,1024]{1,0:T(8,128)S(1)}, u32[]{:S(2)}, u32[]{:S(2)}) collective-permute-start(f32[8,1024]{1,0:T(8,128)S(1)} %get-tuple-element.13.r0_ref), channel_id=1, source_target_pairs={{0,16},{16,0},{32,48},{48,32},{64,80},{80,64},{96,112},{112,96},{1... | collective-permute-start | bytes 98312 | tf_op jit(solution)/shard_map/ppermute | solution.py:307
  53.2 3.6 %collective-permute-start.4 = (f32[8,1024]{1,0:T(8,128)S(1)}, f32[8,1024]{1,0:T(8,128)S(1)}, u32[]{:S(2)}, u32[]{:S(2)}) collective-permute-start(f32[8,1024]{1,0:T(8,128)S(1)} %get-tuple-element.13.r0_ref), channel_id=1, source_target_pairs={{0,32},{16,48},{32,0},{48,16},{64,96},{80,112},{96,64},{112,80},{1... | collective-permute-start | bytes 98312 | tf_op jit(solution)/shard_map/ppermute | solution.py:307
  56.7 2.0 %collective-permute-start.5 = (f32[8,1024]{1,0:T(8,128)S(1)}, f32[8,1024]{1,0:T(8,128)S(1)}, u32[]{:S(2)}, u32[]{:S(2)}) collective-permute-start(f32[8,1024]{1,0:T(8,128)S(1)} %get-tuple-element.13.r0_ref), channel_id=1, source_target_pairs={{0,48},{16,32},{32,16},{48,0},{64,112},{80,96},{96,80},{112,64},{1... | collective-permute-start | bytes 98312 | tf_op jit(solution)/shard_map/ppermute | solution.py:307
  58.7 0.6 collective-permute-done.4.r2_ref
  59.3 2.7 %collective-permute-done.5.r3_ref = f32[8,1024]{1,0:T(8,128)S(1)} collective-permute-done((f32[8,1024]{1,0:T(8,128)S(1)}, f32[8,1024]{1,0:T(8,128)S(1)}, u32[]{:S(2)}, u32[]{:S(2)}) %collective-permute-start.5) | collective-permute-done | bytes 32800 | tf_op jit(solution)/shard_map/ppermute | solution.py:307
  62.0 0.7 assemble.1.after_ref
  62.7 0.7 all-to-all-done.2.message_ref
  63.4 2.3 %grad.1 = f32[32,128]{1,0:T(8,128)S(1)} custom-call(bf16[512,2048]{1,0:T(8,128)(2,1)S(1)} %get-tuple-element.8.masked_ref, bf16[8,64,4096]{2,1,0:T(8,128)(2,1)} %bitcast.13, s32[8,32]{1,0:T(8,128)S(1)} %bitcast.11, s32[32,128]{1,0:T(8,128)S(1)} %bitcast.9, bf16[32,32,128]{2,1,0:T(8,128)(2,1)S(1)} %all-to-all-done.2.message_ref, f32[8,4096]{1,0:T(8,128)} %assemble.1.after_ref), custom_call_target="tpu_custom_call" | custom-call | flops 1073741824 | bytes 5242880 | tf_op jit(solution)/shard_map/grad/pallas_call | solution.py:256
  65.8 19.0 %all_to_all.21 = f16[16,32,128]{2,1,0:T(8,128)(2,1)S(1)} all-to-all(f16[16,32,128]{2,1,0:T(8,128)(2,1)S(1)} %broadcast_in_dim.3), channel_id=1, replica_groups=mesh['orb'=32,'spx'=16] {'spx'}, dimensions={0} | all-to-all | bytes 262144 | tf_op jit(solution)/shard_map/all_to_all | solution.py:321
  84.9 0.6 fusion.1
  (21 shorter events, 0.2 us)
Async XLA Ops:
  0.6 16.4 %copy-start.4 = (bf16[8,4160]{1,0:T(8,128)(2,1)S(1)}, bf16[8,4160]{1,0:T(8,128)(2,1)}, u32[]{:S(2)}) copy-start(bf16[8,4160]{1,0:T(8,128)(2,1)} %t0_ref.1) | copy-start | bytes 199684
  0.6 45.1 %copy-start = (f32[8,4096]{1,0:T(8,128)S(1)}, f32[8,4096]{1,0:T(8,128)}, u32[]{:S(2)}) copy-start(f32[8,4096]{1,0:T(8,128)} %observed_ref.1) | copy-start | bytes 393220
  0.7 45.1 %copy-start.1 = (f32[8,4096]{1,0:T(8,128)S(1)}, f32[8,4096]{1,0:T(8,128)}, u32[]{:S(2)}) copy-start(f32[8,4096]{1,0:T(8,128)} %sigma_ref.1) | copy-start | bytes 393220
  0.7 62.8 %copy-start.2 = (s32[4096]{0:T(1024)S(1)}, s32[4096]{0:T(1024)}, u32[]{:S(2)}) copy-start(s32[4096]{0:T(1024)} %param.10) | copy-start | bytes 49156
  0.7 62.8 %copy-start.3 = (s32[32,8]{0,1:T(8,128)S(1)}, s32[32,8]{0,1:T(8,128)}, u32[]{:S(2)}) copy-start(s32[32,8]{0,1:T(8,128)} %param.9) | copy-start | bytes 3076
  5.4 24.0 %all-to-all-start = ((f16[32,32,128]{2,1,0:T(8,128)(2,1)}), f16[32,32,128]{2,1,0:T(8,128)(2,1)S(1)}, u32[]{:S(2)}, u32[]{:S(2)}) async-start(f16[32,32,128]{2,1,0:T(8,128)(2,1)} %convert_element_type.18), calls=%async_computation | async-start | bytes 524288 | tf_op jit(solution)/shard_map/all_to_all | solution.py:311
  17.0 12.4 %collective-permute-start = (bf16[8,4160]{1,0:T(8,128)(2,1)S(1)}, bf16[8,4160]{1,0:T(8,128)(2,1)S(1)}, u32[]{:S(2)}, u32[]{:S(2)}) collective-permute-start(bf16[8,4160]{1,0:T(8,128)(2,1)S(1)} %copy-done.4), channel_id=1, source_target_pairs={{0,16},{16,0},{32,48},{48,32},{64,80},{80,64},{96,112},{112,96},{1... | collective-permute-start | bytes 199688 | tf_op jit(solution)/shard_map/ppermute | solution.py:307
  19.2 10.3 %collective-permute-start.1 = (bf16[8,4160]{1,0:T(8,128)(2,1)S(1)}, bf16[8,4160]{1,0:T(8,128)(2,1)S(1)}, u32[]{:S(2)}, u32[]{:S(2)}) collective-permute-start(bf16[8,4160]{1,0:T(8,128)(2,1)S(1)} %copy-done.4), channel_id=1, source_target_pairs={{0,32},{16,48},{32,0},{48,16},{64,96},{80,112},{96,64},{112,80},{1... | collective-permute-start | bytes 199688 | tf_op jit(solution)/shard_map/ppermute | solution.py:307
  22.8 6.7 %collective-permute-start.2 = (bf16[8,4160]{1,0:T(8,128)(2,1)S(1)}, bf16[8,4160]{1,0:T(8,128)(2,1)S(1)}, u32[]{:S(2)}, u32[]{:S(2)}) collective-permute-start(bf16[8,4160]{1,0:T(8,128)(2,1)S(1)} %copy-done.4), channel_id=1, source_target_pairs={{0,48},{16,32},{32,16},{48,0},{64,112},{80,96},{96,80},{112,64},{1... | collective-permute-start | bytes 199688 | tf_op jit(solution)/shard_map/ppermute | solution.py:307
  45.8 39.1 %copy-start.5 = (f32[4096]{0:T(1024)S(1)}, f32[4096]{0:T(1024)}, u32[]{:S(2)}) copy-start(f32[4096]{0:T(1024)} %param.7) | copy-start | bytes 49156
  47.2 16.2 %all-to-all-start.2 = ((bf16[32,32,128]{2,1,0:T(8,128)(2,1)}), bf16[32,32,128]{2,1,0:T(8,128)(2,1)S(1)}, u32[]{:S(2)}, u32[]{:S(2)}) async-start(bf16[32,32,128]{2,1,0:T(8,128)(2,1)} %get-tuple-element.12), calls=%async_computation.2 | async-start | bytes 524288 | tf_op jit(solution)/shard_map/all_to_all | solution.py:318
  51.1 7.6 %collective-permute-start.3 = (f32[8,1024]{1,0:T(8,128)S(1)}, f32[8,1024]{1,0:T(8,128)S(1)}, u32[]{:S(2)}, u32[]{:S(2)}) collective-permute-start(f32[8,1024]{1,0:T(8,128)S(1)} %get-tuple-element.13.r0_ref), channel_id=1, source_target_pairs={{0,16},{16,0},{32,48},{48,32},{64,80},{80,64},{96,112},{112,96},{1... | collective-permute-start | bytes 98312 | tf_op jit(solution)/shard_map/ppermute | solution.py:307
  53.2 6.2 %collective-permute-start.4 = (f32[8,1024]{1,0:T(8,128)S(1)}, f32[8,1024]{1,0:T(8,128)S(1)}, u32[]{:S(2)}, u32[]{:S(2)}) collective-permute-start(f32[8,1024]{1,0:T(8,128)S(1)} %get-tuple-element.13.r0_ref), channel_id=1, source_target_pairs={{0,32},{16,48},{32,0},{48,16},{64,96},{80,112},{96,64},{112,80},{1... | collective-permute-start | bytes 98312 | tf_op jit(solution)/shard_map/ppermute | solution.py:307
  56.7 5.3 %collective-permute-start.5 = (f32[8,1024]{1,0:T(8,128)S(1)}, f32[8,1024]{1,0:T(8,128)S(1)}, u32[]{:S(2)}, u32[]{:S(2)}) collective-permute-start(f32[8,1024]{1,0:T(8,128)S(1)} %get-tuple-element.13.r0_ref), channel_id=1, source_target_pairs={{0,48},{16,32},{32,16},{48,0},{64,112},{80,96},{96,80},{112,64},{1... | collective-permute-start | bytes 98312 | tf_op jit(solution)/shard_map/ppermute | solution.py:307

commit v4 on v3

--- a/solution.py
+++ b/solution.py
@@ -6,6 +6,7 @@
 from jax.experimental import pallas as pl
 from jax.experimental.pallas import tpu as pltpu
 from jax.sharding import PartitionSpec as P
+
 
 step_size = 0.5
 
@@ -218,7 +219,7 @@
 
 
 def grad_kernel(
-    masked_ref, losvd_ref, occ_ref, ids_ref, message_ref, after_ref, out_ref, table_ref, rows_ref, sems
+    masked_ref, losvd_ref, occ_ref, ids_ref, message_ref, out_ref, table_ref, rows_ref, sems
 ):
     chunks = 4096 // GRAD_CHUNK
     held = HELD // GRAD_CHUNK
@@ -249,14 +250,14 @@
             out_ref[at : at + 1, :] = jnp.where(gradient < 0.0, -root, root)
 
 
-def grad(masked, losvd, occ, ids, message, after):
+def grad(masked, losvd, occ, ids, message):
     hbm = pl.BlockSpec(memory_space=pltpu.HBM)
     vmem = pl.BlockSpec(memory_space=pltpu.VMEM)
     fetched = max((4096 - HELD) // GRAD_CHUNK, 1)
     return pl.pallas_call(
         grad_kernel,
         name="grad",
-        in_specs=[vmem, hbm, vmem, vmem, vmem, hbm],
+        in_specs=[vmem, hbm, vmem, vmem, vmem],
         out_specs=vmem,
         out_shape=jax.ShapeDtypeStruct((32, LANES), jnp.float32),
         scratch_shapes=[
@@ -266,10 +267,11 @@
         ],
         compiler_params=pltpu.CompilerParams(vmem_limit_bytes=16 << 20),
         cost_estimate=pl.CostEstimate(flops=1 << 30, bytes_accessed=5 << 20, transcendentals=0),
-    )(masked, pltpu.with_memory_space_constraint(losvd, pltpu.HBM), occ, ids, message, pltpu.with_memory_space_constraint(after, pltpu.HBM))
-
-
-def assemble_kernel(r0_ref, r1_ref, r2_ref, r3_ref, out_ref):
+    )(masked, pltpu.with_memory_space_constraint(losvd, pltpu.HBM), occ, ids, message)
+
+
+def finish_kernel(weights_ref, moved_ref, r0_ref, r1_ref, r2_ref, r3_ref, next_ref, out_ref):
+    next_ref[...] = jnp.maximum(weights_ref[...] - step_size * moved_ref[...], 0.0)
     k = whereabouts()
     pieces = [r0_ref[...], r1_ref[...], r2_ref[...], r3_ref[...]]
     for group in range(GROUPS):
@@ -284,15 +286,18 @@
                 ]
 
 
-def assemble(pieces):
-    vmem = pl.BlockSpec(memory_space=pltpu.VMEM)
-    return pl.pallas_call(
-        assemble_kernel,
-        name="assemble",
-        in_specs=[vmem] * 4,
-        out_shape=jax.ShapeDtypeStruct((8, WAVE), jnp.float32),
+def finish(weights, moved, pieces):
+    vmem = pl.BlockSpec(memory_space=pltpu.VMEM)
+    return pl.pallas_call(
+        finish_kernel,
+        name="finish",
+        in_specs=[vmem] * 6,
+        out_shape=[
+            jax.ShapeDtypeStruct((32, LANES), jnp.float32),
+            jax.ShapeDtypeStruct((8, WAVE), jnp.float32),
+        ],
         compiler_params=pltpu.CompilerParams(vmem_limit_bytes=4 << 20),
-    )(*pieces)
+    )(weights, moved, *pieces)
 
 
 def step(weights, losvd, occupancy, template_of, templates, observed, inv_sigma):
@@ -316,11 +321,12 @@
     spectrum = jnp.sum(parts, axis=0) * (1.0 / SPECTRUM_SCALE)
     response, part = respond(spectrum, observed, inv_sigma, wanted)
     message = exchange(response, "orb")
-    residual = assemble([part] + [from_group(part, j) for j in range(1, GROUPS)])
-    roots = grad(masked, rows, occ, ids, message, residual).astype(jnp.float16)
+    pieces = [part] + [from_group(part, j) for j in range(1, GROUPS)]
+    roots = grad(masked, rows, occ, ids, message).astype(jnp.float16)
     sums = exchange(jnp.broadcast_to(roots, (16, 32, LANES)), "spx").astype(jnp.float32)
     moved = jnp.sum(sums * jnp.abs(sums), axis=0) * (1.0 / GRAD_SCALE**2)
-    return jnp.maximum(now - step_size * moved, 0.0).reshape(weights.shape), residual
+    after, residual = finish(now, moved, pieces)
+    return after.reshape(weights.shape), residual
 
 
 def solution(mesh):
@@ -333,4 +339,6 @@
         P("spx", None),
         P("spx", None),
     )
-    return jax.shard_map(step, mesh=mesh, in_specs=placed, out_specs=(P("orb"), P("spx", None)), check_vma=False)
+    return jax.shard_map(
+        step, mesh=mesh, in_specs=placed, out_specs=(P("orb"), P("spx", None)), check_vma=False
+    )

time: 86 us -> 86.7 us (level)
  the two profiles are of different devices: /device:TPU:8 before, /device:TPU:5 now
where the time goes in v4:
time: 86.7 us; the launch traced here: 86.2 us
  starting transfers between devices  38.3 us (44%)
  blocking collectives  29.8 us (34%)
  Pallas kernels  8.7 us (10%)
  waiting for transfers between devices  6.89 us (8%)
  other arithmetic  0.93 us (1%)
  between operations  0.88 us (1%)
    ppermute x6, starting transfers between devices, from_group(): return lax.ppermute(array, 'orb', [(i, i ^ j) for i in range(32)])  17 us
    all_to_all x1, blocking collectives, step(): message = exchange(response, 'orb')  16.3 us
    all_to_all x1, blocking collectives, step(): exchange(sent, 'orb', axis_index_groups=same_spaxels).astype(jnp.float32)  13.6 us
    all_to_all x1, starting transfers between devices, step(): shares = exchange(mixed.astype(jnp.float16), 'orb').astype(jnp.float32)  11.8 us
    all_to_all x1, starting transfers between devices, step(): exchange(jnp.broadcast_to(roots, (16, 32, LANES)), 'spx')  9.52 us
    pallas_call x1, Pallas kernels, mix(): pl.pallas_call(mix_kernel, name='mix', in_specs=[hbm] * 4, out_specs=[vme...  3.91 us
    all_to_all x1, waiting for transfers between devices, step(): shares = exchange(mixed.astype(jnp.float16), 'orb').astype(jnp.float32)  3.53 us
    ppermute x6, waiting for transfers between devices, from_group(): return lax.ppermute(array, 'orb', [(i, i ^ j) for i in range(32)])  3.36 us
  transfers between devices with their start and end apart: 8, of which 3 were waited for; matrix products, arithmetic and copies ran while one was open for 0% of the time, Pallas kernels for 0%

profile of v4, /device:TPU:5, one launch (start us, length us, event | category | flops | bytes accessed | tf_op | source)
XLA Modules:
  0.0 86.2 jit_solution(11121433143029521654)
XLA Ops:
  0.7 3.9 %mix.1 = (f32[32,32,128]{2,1,0:T(8,128)S(1)}, bf16[512,2048]{1,0:T(8,128)(2,1)S(1)}) custom-call(bf16[8,64,4096]{2,1,0:T(8,128)(2,1)} %bitcast.11, s32[8,32]{1,0:T(8,128)} %bitcast.9, s32[32,128]{1,0:T(8,128)} %bitcast.5, f32[32,128]{1,0:T(8,128)} %bitcast.7), custom_call_target="tpu_custom_call" | custom-call | flops 1073741824 | bytes 5242880 | tf_op jit(solution)/shard_map/mix/pallas_call | solution.py:92
  4.6 0.8 convert_element_type.18
  5.4 11.8 %all-to-all-start = ((f16[32,32,128]{2,1,0:T(8,128)(2,1)}), f16[32,32,128]{2,1,0:T(8,128)(2,1)S(1)}, u32[]{:S(2)}, u32[]{:S(2)}) async-start(f16[32,32,128]{2,1,0:T(8,128)(2,1)} %convert_element_type.18), calls=%async_computation | async-start | bytes 524288 | tf_op jit(solution)/shard_map/all_to_all | solution.py:316
  17.1 2.1 %collective-permute-start = (bf16[8,4160]{1,0:T(8,128)(2,1)S(1)}, bf16[8,4160]{1,0:T(8,128)(2,1)S(1)}, u32[]{:S(2)}, u32[]{:S(2)}) collective-permute-start(bf16[8,4160]{1,0:T(8,128)(2,1)S(1)} %copy-done.5), channel_id=1, source_target_pairs={{0,16},{16,0},{32,48},{48,32},{64,80},{80,64},{96,112},{112,96},{1... | collective-permute-start | bytes 199688 | tf_op jit(solution)/shard_map/ppermute | solution.py:312
  19.3 3.4 %collective-permute-start.1 = (bf16[8,4160]{1,0:T(8,128)(2,1)S(1)}, bf16[8,4160]{1,0:T(8,128)(2,1)S(1)}, u32[]{:S(2)}, u32[]{:S(2)}) collective-permute-start(bf16[8,4160]{1,0:T(8,128)(2,1)S(1)} %copy-done.5), channel_id=1, source_target_pairs={{0,32},{16,48},{32,0},{48,16},{64,96},{80,112},{96,64},{112,80},{1... | collective-permute-start | bytes 199688 | tf_op jit(solution)/shard_map/ppermute | solution.py:312
  22.7 2.3 %collective-permute-start.2 = (bf16[8,4160]{1,0:T(8,128)(2,1)S(1)}, bf16[8,4160]{1,0:T(8,128)(2,1)S(1)}, u32[]{:S(2)}, u32[]{:S(2)}) collective-permute-start(bf16[8,4160]{1,0:T(8,128)(2,1)S(1)} %copy-done.5), channel_id=1, source_target_pairs={{0,48},{16,32},{32,16},{48,0},{64,112},{80,96},{96,80},{112,64},{1... | collective-permute-start | bytes 199688 | tf_op jit(solution)/shard_map/ppermute | solution.py:312
  25.0 3.5 %all-to-all-done = f16[32,32,128]{2,1,0:T(8,128)(2,1)S(1)} async-done(((f16[32,32,128]{2,1,0:T(8,128)(2,1)}), f16[32,32,128]{2,1,0:T(8,128)(2,1)S(1)}, u32[]{:S(2)}, u32[]{:S(2)}) %all-to-all-start) | async-done | bytes 262176 | tf_op jit(solution)/shard_map/all_to_all | solution.py:316
  28.6 0.1 multiply_reduce_fusion
  28.6 0.6 collective-permute-done.2.t3_ref
  29.2 1.1 %model.1 = (f32[8,8,1024]{2,1,0:T(8,128)S(1)}, bf16[32,4160]{1,0:T(8,128)(2,1)S(1)}) custom-call(f32[32,128]{1,0:T(8,128)S(1)} %broadcast_multiply_fusion.2.mixture_ref, bf16[8,4160]{1,0:T(8,128)(2,1)S(1)} %copy-done.5, bf16[8,4160]{1,0:T(8,128)(2,1)S(1)} %collective-permute-done.t1_ref, bf16[8,4160]{1,0:T(8,128)(2,1)S(1)} %collective-permute-done.1.t2_ref, ...), custom_call_target="tpu_custom_call" | custom-call | flops 134217728 | bytes 1048576 | tf_op jit(solution)/shard_map/model/pallas_call | solution.py:158
  30.4 13.6 %all_to_all.20 = f16[8,8,1024]{2,1,0:T(8,128)(2,1)S(1)} all-to-all(f16[8,8,1024]{2,1,0:T(8,128)(2,1)S(1)} %multiply_convert_fusion), channel_id=1, replica_groups={{0,64,128,192,256,320,384,448},{16,80,144,208,272,336,400,464},{32,96,1..., dimensions={0} | all-to-all | bytes 262144 | tf_op jit(solution)/shard_map/all_to_all | solution.py:320
  44.0 0.0 copy-start.3
  44.0 0.7 respond.1
  44.7 16.3 %all_to_all.21.message_ref = bf16[32,32,128]{2,1,0:T(8,128)(2,1)S(1)} all-to-all(bf16[32,32,128]{2,1,0:T(8,128)(2,1)S(1)} %get-tuple-element.14), channel_id=1, replica_groups=mesh['orb'=32,'spx'=16] {'orb'}, dimensions={0} | all-to-all | bytes 524288 | tf_op jit(solution)/shard_map/all_to_all | solution.py:323
  61.0 2.3 %grad.1 = f32[32,128]{1,0:T(8,128)S(1)} custom-call(bf16[512,2048]{1,0:T(8,128)(2,1)S(1)} %get-tuple-element.10.masked_ref, bf16[8,64,4096]{2,1,0:T(8,128)(2,1)} %bitcast.12, s32[8,32]{1,0:T(8,128)S(1)} %bitcast.10, s32[32,128]{1,0:T(8,128)S(1)} %bitcast.6, bf16[32,32,128]{2,1,0:T(8,128)(2,1)S(1)} %all_to_all.21.message_ref), custom_call_target="tpu_custom_call" | custom-call | flops 1073741824 | bytes 5242880 | tf_op jit(solution)/shard_map/grad/pallas_call | solution.py:257
  63.3 0.7 broadcast_in_dim.3
  63.9 9.5 %all-to-all-start.3 = ((f16[16,32,128]{2,1,0:T(8,128)(2,1)}), f16[16,32,128]{2,1,0:T(8,128)(2,1)S(1)}, u32[]{:S(2)}, u32[]{:S(2)}) async-start(f16[16,32,128]{2,1,0:T(8,128)(2,1)} %broadcast_in_dim.3), calls=%async_computation.3 | async-start | bytes 262144 | tf_op jit(solution)/shard_map/all_to_all | solution.py:326
  73.5 3.7 %collective-permute-start.3 = (f32[8,1024]{1,0:T(8,128)S(1)}, f32[8,1024]{1,0:T(8,128)S(1)}, u32[]{:S(2)}, u32[]{:S(2)}) collective-permute-start(f32[8,1024]{1,0:T(8,128)S(1)} %get-tuple-element.15.r0_ref), channel_id=1, source_target_pairs={{0,16},{16,0},{32,48},{48,32},{64,80},{80,64},{96,112},{112,96},{1... | collective-permute-start | bytes 98312 | tf_op jit(solution)/shard_map/ppermute | solution.py:312
  77.2 3.1 %collective-permute-start.4 = (f32[8,1024]{1,0:T(8,128)S(1)}, f32[8,1024]{1,0:T(8,128)S(1)}, u32[]{:S(2)}, u32[]{:S(2)}) collective-permute-start(f32[8,1024]{1,0:T(8,128)S(1)} %get-tuple-element.15.r0_ref), channel_id=1, source_target_pairs={{0,32},{16,48},{32,0},{48,16},{64,96},{80,112},{96,64},{112,80},{1... | collective-permute-start | bytes 98312 | tf_op jit(solution)/shard_map/ppermute | solution.py:312
  80.3 2.4 %collective-permute-start.5 = (f32[8,1024]{1,0:T(8,128)S(1)}, f32[8,1024]{1,0:T(8,128)S(1)}, u32[]{:S(2)}, u32[]{:S(2)}) collective-permute-start(f32[8,1024]{1,0:T(8,128)S(1)} %get-tuple-element.15.r0_ref), channel_id=1, source_target_pairs={{0,48},{16,32},{32,16},{48,0},{64,112},{80,96},{96,80},{112,64},{1... | collective-permute-start | bytes 98312 | tf_op jit(solution)/shard_map/ppermute | solution.py:312
  82.6 0.0 all-to-all-done.3
  82.7 0.0 collective-permute-done.3.r1_ref
  82.7 2.8 %collective-permute-done.5.r3_ref = f32[8,1024]{1,0:T(8,128)S(1)} collective-permute-done((f32[8,1024]{1,0:T(8,128)S(1)}, f32[8,1024]{1,0:T(8,128)S(1)}, u32[]{:S(2)}, u32[]{:S(2)}) %collective-permute-start.5) | collective-permute-done | bytes 32800 | tf_op jit(solution)/shard_map/ppermute | solution.py:312
  85.5 0.7 finish.1
  (21 shorter events, 0.1 us)
Async XLA Ops:
  0.6 60.3 %copy-start.4 = (s32[32,8]{0,1:T(8,128)S(1)}, s32[32,8]{0,1:T(8,128)}, u32[]{:S(2)}) copy-start(s32[32,8]{0,1:T(8,128)} %param.9) | copy-start | bytes 3076
  0.6 60.3 %copy-start.2 = (s32[4096]{0:T(1024)S(1)}, s32[4096]{0:T(1024)}, u32[]{:S(2)}) copy-start(s32[4096]{0:T(1024)} %param.10) | copy-start | bytes 49156
  0.7 16.5 %copy-start.5 = (bf16[8,4160]{1,0:T(8,128)(2,1)S(1)}, bf16[8,4160]{1,0:T(8,128)(2,1)}, u32[]{:S(2)}) copy-start(bf16[8,4160]{1,0:T(8,128)(2,1)} %t0_ref.1) | copy-start | bytes 199684
  0.7 43.3 %copy-start = (f32[8,4096]{1,0:T(8,128)S(1)}, f32[8,4096]{1,0:T(8,128)}, u32[]{:S(2)}) copy-start(f32[8,4096]{1,0:T(8,128)} %observed_ref.1) | copy-start | bytes 393220
  0.7 43.3 %copy-start.1 = (f32[8,4096]{1,0:T(8,128)S(1)}, f32[8,4096]{1,0:T(8,128)}, u32[]{:S(2)}) copy-start(f32[8,4096]{1,0:T(8,128)} %sigma_ref.1) | copy-start | bytes 393220
  5.4 23.2 %all-to-all-start = ((f16[32,32,128]{2,1,0:T(8,128)(2,1)}), f16[32,32,128]{2,1,0:T(8,128)(2,1)S(1)}, u32[]{:S(2)}, u32[]{:S(2)}) async-start(f16[32,32,128]{2,1,0:T(8,128)(2,1)} %convert_element_type.18), calls=%async_computation | async-start | bytes 524288 | tf_op jit(solution)/shard_map/all_to_all | solution.py:316
  17.1 11.5 %collective-permute-start = (bf16[8,4160]{1,0:T(8,128)(2,1)S(1)}, bf16[8,4160]{1,0:T(8,128)(2,1)S(1)}, u32[]{:S(2)}, u32[]{:S(2)}) collective-permute-start(bf16[8,4160]{1,0:T(8,128)(2,1)S(1)} %copy-done.5), channel_id=1, source_target_pairs={{0,16},{16,0},{32,48},{48,32},{64,80},{80,64},{96,112},{112,96},{1... | collective-permute-start | bytes 199688 | tf_op jit(solution)/shard_map/ppermute | solution.py:312
  19.3 9.4 %collective-permute-start.1 = (bf16[8,4160]{1,0:T(8,128)(2,1)S(1)}, bf16[8,4160]{1,0:T(8,128)(2,1)S(1)}, u32[]{:S(2)}, u32[]{:S(2)}) collective-permute-start(bf16[8,4160]{1,0:T(8,128)(2,1)S(1)} %copy-done.5), channel_id=1, source_target_pairs={{0,32},{16,48},{32,0},{48,16},{64,96},{80,112},{96,64},{112,80},{1... | collective-permute-start | bytes 199688 | tf_op jit(solution)/shard_map/ppermute | solution.py:312
  22.7 6.5 %collective-permute-start.2 = (bf16[8,4160]{1,0:T(8,128)(2,1)S(1)}, bf16[8,4160]{1,0:T(8,128)(2,1)S(1)}, u32[]{:S(2)}, u32[]{:S(2)}) collective-permute-start(bf16[8,4160]{1,0:T(8,128)(2,1)S(1)} %copy-done.5), channel_id=1, source_target_pairs={{0,48},{16,32},{32,16},{48,0},{64,112},{80,96},{96,80},{112,64},{1... | collective-permute-start | bytes 199688 | tf_op jit(solution)/shard_map/ppermute | solution.py:312
  44.0 41.6 %copy-start.3 = (f32[4096]{0:T(1024)S(1)}, f32[4096]{0:T(1024)}, u32[]{:S(2)}) copy-start(f32[4096]{0:T(1024)} %param.7) | copy-start | bytes 49156
  63.9 18.7 %all-to-all-start.3 = ((f16[16,32,128]{2,1,0:T(8,128)(2,1)}), f16[16,32,128]{2,1,0:T(8,128)(2,1)S(1)}, u32[]{:S(2)}, u32[]{:S(2)}) async-start(f16[16,32,128]{2,1,0:T(8,128)(2,1)} %broadcast_in_dim.3), calls=%async_computation.3 | async-start | bytes 262144 | tf_op jit(solution)/shard_map/all_to_all | solution.py:326
  73.5 9.2 %collective-permute-start.3 = (f32[8,1024]{1,0:T(8,128)S(1)}, f32[8,1024]{1,0:T(8,128)S(1)}, u32[]{:S(2)}, u32[]{:S(2)}) collective-permute-start(f32[8,1024]{1,0:T(8,128)S(1)} %get-tuple-element.15.r0_ref), channel_id=1, source_target_pairs={{0,16},{16,0},{32,48},{48,32},{64,80},{80,64},{96,112},{112,96},{1... | collective-permute-start | bytes 98312 | tf_op jit(solution)/shard_map/ppermute | solution.py:312
  77.2 5.6 %collective-permute-start.4 = (f32[8,1024]{1,0:T(8,128)S(1)}, f32[8,1024]{1,0:T(8,128)S(1)}, u32[]{:S(2)}, u32[]{:S(2)}) collective-permute-start(f32[8,1024]{1,0:T(8,128)S(1)} %get-tuple-element.15.r0_ref), channel_id=1, source_target_pairs={{0,32},{16,48},{32,0},{48,16},{64,96},{80,112},{96,64},{112,80},{1... | collective-permute-start | bytes 98312 | tf_op jit(solution)/shard_map/ppermute | solution.py:312
  80.3 5.2 %collective-permute-start.5 = (f32[8,1024]{1,0:T(8,128)S(1)}, f32[8,1024]{1,0:T(8,128)S(1)}, u32[]{:S(2)}, u32[]{:S(2)}) collective-permute-start(f32[8,1024]{1,0:T(8,128)S(1)} %get-tuple-element.15.r0_ref), channel_id=1, source_target_pairs={{0,48},{16,32},{32,16},{48,0},{64,112},{80,96},{96,80},{112,64},{1... | collective-permute-start | bytes 98312 | tf_op jit(solution)/shard_map/ppermute | solution.py:312

commit v5 on v4

--- a/solution.py
+++ b/solution.py
@@ -20,7 +20,7 @@
 TEMPL = 256
 PAIR = 128
 MIX_CHUNK = 1024
-HELD = 2048
+HELD = 3072
 GRAD_CHUNK = 1024
 MIX_SCALE = 8192.0
 GRAD_SCALE = 16.0
@@ -311,7 +311,9 @@
     def from_group(array, j):
         return lax.ppermute(array, "orb", [(i, i ^ j) for i in range(32)])
 
-    gathered = [templates] + [from_group(templates, j) for j in range(1, GROUPS)]
+    gathered = [templates]
+    for j in range(1, GROUPS):
+        gathered.append(from_group(templates, j))
     mixed, masked = mix(rows, occ, ids, now)
     shares = exchange(mixed.astype(jnp.float16), "orb").astype(jnp.float32)
     mixture = jnp.sum(shares * shares, axis=0) * (1.0 / MIX_SCALE**2)

time: 86.7 us -> 87.5 us (level)
  other arithmetic: 0.93 us -> 1.87 us
    reduce_sum x1, other arithmetic: 0.07 us -> 1.02 us  [step(): mixture = jnp.sum(shares * shares, axis=0) * (1.0 / MIX_SCALE ** 2)]
    pallas_call x1, Pallas kernels: 1.09 us -> 2.04 us  [model(): pl.pallas_call(model_kernel, name='model', in_specs=[vmem] * 5, out_shape...]
  transfers between devices with their start and end apart: 8 -> 8, of which waited for: 3 -> 2; matrix products, arithmetic and copies ran while one was open for 0% -> 1% of each run, Pallas kernels for 0% -> 0%
where the time goes in v5:
time: 87.5 us; the launch traced here: 86.9 us
  starting transfers between devices  38.4 us (44%)
  blocking collectives  29.5 us (34%)
  Pallas kernels  9.2 us (11%)
  waiting for transfers between devices  6.37 us (7%)
  other arithmetic  1.87 us (2%)
    ppermute x6, starting transfers between devices, from_group(): return lax.ppermute(array, 'orb', [(i, i ^ j) for i in range(32)])  17 us
    all_to_all x1, blocking collectives, step(): message = exchange(response, 'orb')  16.3 us
    all_to_all x1, blocking collectives, step(): exchange(sent, 'orb', axis_index_groups=same_spaxels).astype(jnp.float32)  13.2 us
    all_to_all x1, starting transfers between devices, step(): shares = exchange(mixed.astype(jnp.float16), 'orb').astype(jnp.float32)  11.8 us
    all_to_all x1, starting transfers between devices, step(): exchange(jnp.broadcast_to(roots, (16, 32, LANES)), 'spx')  9.53 us
    pallas_call x1, Pallas kernels, mix(): pl.pallas_call(mix_kernel, name='mix', in_specs=[hbm] * 4, out_specs=[vme...  3.95 us
    all_to_all x1, waiting for transfers between devices, step(): shares = exchange(mixed.astype(jnp.float16), 'orb').astype(jnp.float32)  3.57 us
    ppermute x6, waiting for transfers between devices, from_group(): return lax.ppermute(array, 'orb', [(i, i ^ j) for i in range(32)])  2.79 us
  transfers between devices with their start and end apart: 8, of which 2 were waited for; matrix products, arithmetic and copies ran while one was open for 1% of the time, Pallas kernels for 0%

profile of v5, /device:TPU:5, one launch (start us, length us, event | category | flops | bytes accessed | tf_op | source)
XLA Modules:
  0.0 86.9 jit_solution(14462993738492356517)
XLA Ops:
  0.7 3.9 %mix.1 = (f32[32,32,128]{2,1,0:T(8,128)S(1)}, bf16[512,3072]{1,0:T(8,128)(2,1)S(1)}) custom-call(bf16[8,64,4096]{2,1,0:T(8,128)(2,1)} %bitcast.11, s32[8,32]{1,0:T(8,128)} %bitcast.9, s32[32,128]{1,0:T(8,128)} %bitcast.5, f32[32,128]{1,0:T(8,128)} %bitcast.7), custom_call_target="tpu_custom_call" | custom-call | flops 1073741824 | bytes 5242880 | tf_op jit(solution)/shard_map/mix/pallas_call | solution.py:92
  4.6 0.7 convert_element_type.18
  5.4 11.8 %all-to-all-start = ((f16[32,32,128]{2,1,0:T(8,128)(2,1)}), f16[32,32,128]{2,1,0:T(8,128)(2,1)}, u32[]{:S(2)}, u32[]{:S(2)}) async-start(f16[32,32,128]{2,1,0:T(8,128)(2,1)} %convert_element_type.18), calls=%async_computation | async-start | bytes 524288 | tf_op jit(solution)/shard_map/all_to_all | solution.py:318
  17.2 2.2 %collective-permute-start = (bf16[8,4160]{1,0:T(8,128)(2,1)S(1)}, bf16[8,4160]{1,0:T(8,128)(2,1)}, u32[]{:S(2)}, u32[]{:S(2)}) collective-permute-start(bf16[8,4160]{1,0:T(8,128)(2,1)S(1)} %copy-done.5), channel_id=1, source_target_pairs={{0,16},{16,0},{32,48},{48,32},{64,80},{80,64},{96,112},{112,96},{1... | collective-permute-start | bytes 199688 | tf_op jit(solution)/shard_map/ppermute | solution.py:312
  19.4 3.3 %collective-permute-start.1 = (bf16[8,4160]{1,0:T(8,128)(2,1)S(1)}, bf16[8,4160]{1,0:T(8,128)(2,1)}, u32[]{:S(2)}, u32[]{:S(2)}) collective-permute-start(bf16[8,4160]{1,0:T(8,128)(2,1)S(1)} %copy-done.5), channel_id=1, source_target_pairs={{0,32},{16,48},{32,0},{48,16},{64,96},{80,112},{96,64},{112,80},{1... | collective-permute-start | bytes 199688 | tf_op jit(solution)/shard_map/ppermute | solution.py:312
  22.8 2.3 %collective-permute-start.2 = (bf16[8,4160]{1,0:T(8,128)(2,1)S(1)}, bf16[8,4160]{1,0:T(8,128)(2,1)}, u32[]{:S(2)}, u32[]{:S(2)}) collective-permute-start(bf16[8,4160]{1,0:T(8,128)(2,1)S(1)} %copy-done.5), channel_id=1, source_target_pairs={{0,48},{16,32},{32,16},{48,0},{64,112},{80,96},{96,80},{112,64},{1... | collective-permute-start | bytes 199688 | tf_op jit(solution)/shard_map/ppermute | solution.py:312
  25.1 3.6 %all-to-all-done = f16[32,32,128]{2,1,0:T(8,128)(2,1)} async-done(((f16[32,32,128]{2,1,0:T(8,128)(2,1)}), f16[32,32,128]{2,1,0:T(8,128)(2,1)}, u32[]{:S(2)}, u32[]{:S(2)}) %all-to-all-start) | async-done | bytes 262176 | tf_op jit(solution)/shard_map/all_to_all | solution.py:318
  28.7 1.0 %multiply_reduce_fusion = f32[32,128]{1,0:T(8,128)S(1)} fusion(f16[32,32,128]{2,1,0:T(8,128)(2,1)} %all-to-all-done), kind=kLoop, calls=%fused_computation | loop fusion | flops 389120 | bytes 278528 | tf_op jit(solution)/shard_map/reduce_sum | solution.py:319
  29.7 0.0 collective-permute-done.t1_ref
  29.7 0.0 collective-permute-done.1.t2_ref
  29.7 0.0 collective-permute-done.2.t3_ref
  29.7 2.0 %model.1 = (f32[8,8,1024]{2,1,0:T(8,128)S(1)}, bf16[32,4160]{1,0:T(8,128)(2,1)S(1)}) custom-call(f32[32,128]{1,0:T(8,128)S(1)} %broadcast_multiply_fusion.2.mixture_ref, bf16[8,4160]{1,0:T(8,128)(2,1)S(1)} %copy-done.5, bf16[8,4160]{1,0:T(8,128)(2,1)} %collective-permute-done.t1_ref, bf16[8,4160]{1,0:T(8,128)(2,1)} %collective-permute-done.1.t2_ref, ...), custom_call_target="tpu_custom_call" | custom-call | flops 134217728 | bytes 1048576 | tf_op jit(solution)/shard_map/model/pallas_call | solution.py:158
  31.8 13.2 %all_to_all.20 = f16[8,8,1024]{2,1,0:T(8,128)(2,1)S(1)} all-to-all(f16[8,8,1024]{2,1,0:T(8,128)(2,1)S(1)} %multiply_convert_fusion), channel_id=1, replica_groups={{0,64,128,192,256,320,384,448},{16,80,144,208,272,336,400,464},{32,96,1..., dimensions={0} | all-to-all | bytes 262144 | tf_op jit(solution)/shard_map/all_to_all | solution.py:322
  45.1 0.7 respond.1
  45.8 16.3 %all_to_all.21.message_ref = bf16[32,32,128]{2,1,0:T(8,128)(2,1)S(1)} all-to-all(bf16[32,32,128]{2,1,0:T(8,128)(2,1)S(1)} %get-tuple-element.14), channel_id=1, replica_groups=mesh['orb'=32,'spx'=16] {'orb'}, dimensions={0} | all-to-all | bytes 524288 | tf_op jit(solution)/shard_map/all_to_all | solution.py:325
  62.1 1.8 %grad.1 = f32[32,128]{1,0:T(8,128)S(1)} custom-call(bf16[512,3072]{1,0:T(8,128)(2,1)S(1)} %get-tuple-element.10.masked_ref, bf16[8,64,4096]{2,1,0:T(8,128)(2,1)} %bitcast.12, s32[8,32]{1,0:T(8,128)S(1)} %bitcast.10, s32[32,128]{1,0:T(8,128)S(1)} %bitcast.6, bf16[32,32,128]{2,1,0:T(8,128)(2,1)S(1)} %all_to_all.21.message_ref), custom_call_target="tpu_custom_call" | custom-call | flops 1073741824 | bytes 5242880 | tf_op jit(solution)/shard_map/grad/pallas_call | solution.py:257
  63.9 0.7 broadcast_in_dim.3
  64.6 9.5 %all-to-all-start.3 = ((f16[16,32,128]{2,1,0:T(8,128)(2,1)}), f16[16,32,128]{2,1,0:T(8,128)(2,1)S(1)}, u32[]{:S(2)}, u32[]{:S(2)}) async-start(f16[16,32,128]{2,1,0:T(8,128)(2,1)} %broadcast_in_dim.3), calls=%async_computation.3 | async-start | bytes 262144 | tf_op jit(solution)/shard_map/all_to_all | solution.py:328
  74.1 3.7 %collective-permute-start.3 = (f32[8,1024]{1,0:T(8,128)S(1)}, f32[8,1024]{1,0:T(8,128)S(1)}, u32[]{:S(2)}, u32[]{:S(2)}) collective-permute-start(f32[8,1024]{1,0:T(8,128)S(1)} %get-tuple-element.15.r0_ref), channel_id=1, source_target_pairs={{0,16},{16,0},{32,48},{48,32},{64,80},{80,64},{96,112},{112,96},{1... | collective-permute-start | bytes 98312 | tf_op jit(solution)/shard_map/ppermute | solution.py:312
  77.8 3.1 %collective-permute-start.4 = (f32[8,1024]{1,0:T(8,128)S(1)}, f32[8,1024]{1,0:T(8,128)S(1)}, u32[]{:S(2)}, u32[]{:S(2)}) collective-permute-start(f32[8,1024]{1,0:T(8,128)S(1)} %get-tuple-element.15.r0_ref), channel_id=1, source_target_pairs={{0,32},{16,48},{32,0},{48,16},{64,96},{80,112},{96,64},{112,80},{1... | collective-permute-start | bytes 98312 | tf_op jit(solution)/shard_map/ppermute | solution.py:312
  80.9 2.4 %collective-permute-start.5 = (f32[8,1024]{1,0:T(8,128)S(1)}, f32[8,1024]{1,0:T(8,128)S(1)}, u32[]{:S(2)}, u32[]{:S(2)}) collective-permute-start(f32[8,1024]{1,0:T(8,128)S(1)} %get-tuple-element.15.r0_ref), channel_id=1, source_target_pairs={{0,48},{16,32},{32,16},{48,0},{64,112},{80,96},{96,80},{112,64},{1... | collective-permute-start | bytes 98312 | tf_op jit(solution)/shard_map/ppermute | solution.py:312
  83.3 0.0 all-to-all-done.3
  83.4 2.8 %collective-permute-done.5.r3_ref = f32[8,1024]{1,0:T(8,128)S(1)} collective-permute-done((f32[8,1024]{1,0:T(8,128)S(1)}, f32[8,1024]{1,0:T(8,128)S(1)}, u32[]{:S(2)}, u32[]{:S(2)}) %collective-permute-start.5) | collective-permute-done | bytes 32800 | tf_op jit(solution)/shard_map/ppermute | solution.py:312
  86.2 0.7 finish.1
  (21 shorter events, 0.1 us)
Async XLA Ops:
  0.6 61.5 %copy-start.4 = (s32[32,8]{0,1:T(8,128)S(1)}, s32[32,8]{0,1:T(8,128)}, u32[]{:S(2)}) copy-start(s32[32,8]{0,1:T(8,128)} %param.9) | copy-start | bytes 3076
  0.6 61.5 %copy-start.2 = (s32[4096]{0:T(1024)S(1)}, s32[4096]{0:T(1024)}, u32[]{:S(2)}) copy-start(s32[4096]{0:T(1024)} %param.10) | copy-start | bytes 49156
  0.7 16.6 %copy-start.5 = (bf16[8,4160]{1,0:T(8,128)(2,1)S(1)}, bf16[8,4160]{1,0:T(8,128)(2,1)}, u32[]{:S(2)}) copy-start(bf16[8,4160]{1,0:T(8,128)(2,1)} %t0_ref.1) | copy-start | bytes 199684
  0.7 44.4 %copy-start = (f32[8,4096]{1,0:T(8,128)S(1)}, f32[8,4096]{1,0:T(8,128)}, u32[]{:S(2)}) copy-start(f32[8,4096]{1,0:T(8,128)} %observed_ref.1) | copy-start | bytes 393220
  0.7 44.4 %copy-start.1 = (f32[8,4096]{1,0:T(8,128)S(1)}, f32[8,4096]{1,0:T(8,128)}, u32[]{:S(2)}) copy-start(f32[8,4096]{1,0:T(8,128)} %sigma_ref.1) | copy-start | bytes 393220
  5.4 23.3 %all-to-all-start = ((f16[32,32,128]{2,1,0:T(8,128)(2,1)}), f16[32,32,128]{2,1,0:T(8,128)(2,1)}, u32[]{:S(2)}, u32[]{:S(2)}) async-start(f16[32,32,128]{2,1,0:T(8,128)(2,1)} %convert_element_type.18), calls=%async_computation | async-start | bytes 524288 | tf_op jit(solution)/shard_map/all_to_all | solution.py:318
  17.2 12.5 %collective-permute-start = (bf16[8,4160]{1,0:T(8,128)(2,1)S(1)}, bf16[8,4160]{1,0:T(8,128)(2,1)}, u32[]{:S(2)}, u32[]{:S(2)}) collective-permute-start(bf16[8,4160]{1,0:T(8,128)(2,1)S(1)} %copy-done.5), channel_id=1, source_target_pairs={{0,16},{16,0},{32,48},{48,32},{64,80},{80,64},{96,112},{112,96},{1... | collective-permute-start | bytes 199688 | tf_op jit(solution)/shard_map/ppermute | solution.py:312
  19.4 10.3 %collective-permute-start.1 = (bf16[8,4160]{1,0:T(8,128)(2,1)S(1)}, bf16[8,4160]{1,0:T(8,128)(2,1)}, u32[]{:S(2)}, u32[]{:S(2)}) collective-permute-start(bf16[8,4160]{1,0:T(8,128)(2,1)S(1)} %copy-done.5), channel_id=1, source_target_pairs={{0,32},{16,48},{32,0},{48,16},{64,96},{80,112},{96,64},{112,80},{1... | collective-permute-start | bytes 199688 | tf_op jit(solution)/shard_map/ppermute | solution.py:312
  22.8 6.9 %collective-permute-start.2 = (bf16[8,4160]{1,0:T(8,128)(2,1)S(1)}, bf16[8,4160]{1,0:T(8,128)(2,1)}, u32[]{:S(2)}, u32[]{:S(2)}) collective-permute-start(bf16[8,4160]{1,0:T(8,128)(2,1)S(1)} %copy-done.5), channel_id=1, source_target_pairs={{0,48},{16,32},{32,16},{48,0},{64,112},{80,96},{96,80},{112,64},{1... | collective-permute-start | bytes 199688 | tf_op jit(solution)/shard_map/ppermute | solution.py:312
  62.1 24.1 %copy-start.3 = (f32[4096]{0:T(1024)S(1)}, f32[4096]{0:T(1024)}, u32[]{:S(2)}) copy-start(f32[4096]{0:T(1024)} %param.7) | copy-start | bytes 49156
  64.6 18.7 %all-to-all-start.3 = ((f16[16,32,128]{2,1,0:T(8,128)(2,1)}), f16[16,32,128]{2,1,0:T(8,128)(2,1)S(1)}, u32[]{:S(2)}, u32[]{:S(2)}) async-start(f16[16,32,128]{2,1,0:T(8,128)(2,1)} %broadcast_in_dim.3), calls=%async_computation.3 | async-start | bytes 262144 | tf_op jit(solution)/shard_map/all_to_all | solution.py:328
  74.1 9.2 %collective-permute-start.3 = (f32[8,1024]{1,0:T(8,128)S(1)}, f32[8,1024]{1,0:T(8,128)S(1)}, u32[]{:S(2)}, u32[]{:S(2)}) collective-permute-start(f32[8,1024]{1,0:T(8,128)S(1)} %get-tuple-element.15.r0_ref), channel_id=1, source_target_pairs={{0,16},{16,0},{32,48},{48,32},{64,80},{80,64},{96,112},{112,96},{1... | collective-permute-start | bytes 98312 | tf_op jit(solution)/shard_map/ppermute | solution.py:312
  77.8 5.6 %collective-permute-start.4 = (f32[8,1024]{1,0:T(8,128)S(1)}, f32[8,1024]{1,0:T(8,128)S(1)}, u32[]{:S(2)}, u32[]{:S(2)}) collective-permute-start(f32[8,1024]{1,0:T(8,128)S(1)} %get-tuple-element.15.r0_ref), channel_id=1, source_target_pairs={{0,32},{16,48},{32,0},{48,16},{64,96},{80,112},{96,64},{112,80},{1... | collective-permute-start | bytes 98312 | tf_op jit(solution)/shard_map/ppermute | solution.py:312
  80.9 5.2 %collective-permute-start.5 = (f32[8,1024]{1,0:T(8,128)S(1)}, f32[8,1024]{1,0:T(8,128)S(1)}, u32[]{:S(2)}, u32[]{:S(2)}) collective-permute-start(f32[8,1024]{1,0:T(8,128)S(1)} %get-tuple-element.15.r0_ref), channel_id=1, source_target_pairs={{0,48},{16,32},{32,16},{48,0},{64,112},{80,96},{96,80},{112,64},{1... | collective-permute-start | bytes 98312 | tf_op jit(solution)/shard_map/ppermute | solution.py:312
